TPU v7x, 32 devices: a whole 2x2x4 slice. The times are simulated.
32 devices in a mesh: gx: 4 (over z), gy: 4 (over y, x), ma: 2 (over core).
Axes of the slice: x: 2, y: 2, z: 4, core: 2. Of those that a mesh axis runs over, the one named last changes fastest.
Arguments:
- perturbations: float32 [30, 2, 128, 2048], P('ma', None, 'gx', 'gy'), may hold values from -6 to 6
- coefficients: float32 [2, 128, 2048], P(None, 'gx', 'gy'), may hold values from 0.02 to 0.12
- coarse_coefficients: float32 [2, 32, 512], P(None, 'gx', 'gy'), may hold values from 0.02 to 0.12
- iterate: float32 [2, 128, 2048], P(None, 'gx', 'gy'), may hold values from -6 to 6
- residual: float32 [2, 128, 2048], P(None, 'gx', 'gy'), may hold values from -6 to 6
- direction: float32 [2, 128, 2048], P(None, 'gx', 'gy'), may hold values from -6 to 6
Outputs:
- new_iterate: float32 [2, 128, 2048], P(None, 'gx', 'gy')
- new_residual: float32 [2, 128, 2048], P(None, 'gx', 'gy')
- new_direction: float32 [2, 128, 2048], P(None, 'gx', 'gy')
All inputs are finite; a program needn't handle non-finite values.
Results may differ from a plain program's by a relative error of at most 0.0001.
Values sent between devices are 32-bit elements; how exact they have to be, the bound alone decides.
A program may use at most 192 MiB of HBM per device.

v0:
```python
import jax
import jax.numpy as jnp
from jax import lax
from jax.sharding import PartitionSpec as P

MEMBERS = 30
PASSES = 3
RATIO = 4


def padded(cells, sides, width):
    for axis, dim in sides:
        count = lax.axis_size(axis)
        ends = count - 1
        head = lax.slice_in_dim(cells, 0, width, axis=dim)
        tail = lax.slice_in_dim(cells, cells.shape[dim] - width, cells.shape[dim], axis=dim)
        cells = jnp.concatenate(
            [
                lax.ppermute(tail, axis, [(i, (i + 1) % count) for i in range(ends)]),
                cells,
                lax.ppermute(head, axis, [((i + 1) % count, i) for i in range(ends)]),
            ],
            axis=dim,
        )
    return cells


def stencil_pass(source, coef_x, coef_y):
    centre = source[..., 1:-1, 1:-1]
    edge_x = 0.5 * (coef_x[1:, 1:-1] + coef_x[:-1, 1:-1])
    edge_y = 0.5 * (coef_y[1:-1, 1:] + coef_y[1:-1, :-1])
    along_x = edge_x[1:] * (source[..., 2:, 1:-1] - centre) - edge_x[:-1] * (
        centre - source[..., :-2, 1:-1]
    )
    along_y = edge_y[:, 1:] * (source[..., 1:-1, 2:] - centre) - edge_y[:, :-1] * (
        centre - source[..., 1:-1, :-2]
    )
    return centre + along_x + along_y


def smooth_level(source, extended_coefs, extend):
    coef_rows = extended_coefs.shape[1]
    coef_cols = extended_coefs.shape[2]
    trimmed = PASSES - 1
    coef_x = extended_coefs[0, trimmed : coef_rows - trimmed, trimmed : coef_cols - trimmed]
    coef_y = extended_coefs[1, trimmed : coef_rows - trimmed, trimmed : coef_cols - trimmed]
    result = source
    for sweep_index in range(PASSES):
        result = stencil_pass(extend(result, 1), coef_x, coef_y)
    return result


def restrict_blocks(source):
    shaped = source.reshape(
        source.shape[:-2] + (source.shape[-2] // RATIO, RATIO, source.shape[-1] // RATIO, RATIO)
    )
    return jnp.mean(shaped, axis=(-3, -1))


def prolong_blocks(source):
    return jnp.repeat(jnp.repeat(source, RATIO, axis=-2), RATIO, axis=-1)


def fine_extend(values, margin):
    return padded(values, (("gx", 2), ("gy", 3)), margin)


def coarse_extend(values, margin):
    return padded(values, (("gx", 2), ("gy", 3)), margin)


def local(perturbations, coefficients, coarse_coefficients, iterate, residual, direction):
    fine_coefs = padded(coefficients, (("gx", 1), ("gy", 2)), PASSES)
    weighted = perturbations * direction[None]
    fine_part = smooth_level(weighted, fine_coefs, fine_extend)
    coarse_field = restrict_blocks(weighted)
    sharded_coefs = padded(coarse_coefficients, (("gx", 1), ("gy", 2)), PASSES)
    coarse_part = smooth_level(coarse_field, sharded_coefs, coarse_extend)
    localized = fine_part + prolong_blocks(coarse_part)
    partial_value = jnp.sum(perturbations * localized, axis=0) / (MEMBERS - 1)
    operator_image = direction + lax.psum(partial_value, "ma")
    norm_old = lax.psum(jnp.sum(residual * residual), ("gx", "gy"))
    curvature = lax.psum(jnp.sum(direction * operator_image), ("gx", "gy"))
    step_length = norm_old / curvature
    new_iterate = iterate + step_length * direction
    new_residual = residual - step_length * operator_image
    norm_new = lax.psum(jnp.sum(new_residual * new_residual), ("gx", "gy"))
    new_direction = new_residual + norm_new / norm_old * direction
    return (new_iterate, new_residual, new_direction)


def solution(mesh):
    placed = (
        P("ma", None, "gx", "gy"),
        P(None, "gx", "gy"),
        P(None, "gx", "gy"),
        P(None, "gx", "gy"),
        P(None, "gx", "gy"),
        P(None, "gx", "gy"),
    )
    return jax.shard_map(
        local,
        mesh=mesh,
        in_specs=placed,
        out_specs=(P(None, "gx", "gy"), P(None, "gx", "gy"), P(None, "gx", "gy")),
        check_vma=False,
    )
```

profile of v0, /device:TPU:0, one launch (start us, length us, event | category | flops | bytes accessed | tf_op | source)
XLA Modules:
  0.0 549.8 jit_solution(2422610982305113034)
XLA Ops:
  7.2 6.0 %copy.255 = f32[15,2,32,512]{2,3,1,0:T(8,128)} copy(f32[15,2,32,512]{3,2,1,0:T(8,128)} %param.6) | data formatting | bytes 3932160 | tf_op args[0]
  13.5 7.1 %broadcast_multiply_fusion = f32[15,2,32,512]{2,3,1,0:T(8,128)} fusion(f32[15,2,32,512]{2,3,1,0:T(8,128)} %copy.255, f32[2,32,512]{1,2,0:T(8,128)S(1)} %copy.210), kind=kLoop, calls=%fused_computation.30 | loop fusion | flops 491520 | bytes 4063232 | tf_op jit(solution)/shard_map/mul | solution.py:74
  20.6 16.6 %copy.237 = f32[15,2,32,512]{0,3,2,1:T(8,128)} copy(f32[15,2,32,512]{2,3,1,0:T(8,128)} %broadcast_multiply_fusion) | data formatting | bytes 3932160 | tf_op jit(solution)/shard_map/mul | solution.py:74
  37.2 10.1 %reduce_sum.46 = f32[15,2,8,128]{0,3,2,1:T(8,128)S(1)} reduce(f32[15,2,8,4,128,4]{0,5,4,3,2,1:T(4,128)} %bitcast.17, f32[]{:T(128)} %constant.4.clone.1), dimensions={3,5}, to_apply=%region_2.0 | reduce | flops 460800 | bytes 2088964 | tf_op jit(solution)/shard_map/reduce_sum | solution.py:57
  60.4 13.1 %fusion.60 = (f32[15,2,1,512]{2,3,1,0:T(8,128)}, f32[15,2,1,512]{2,3,1,0:T(8,128)}) fusion(f32[15,2,32,512]{2,3,1,0:T(8,128)} %broadcast_multiply_fusion), kind=kLoop, calls=%fused_computation.149 | loop fusion | bytes 245760 | tf_op jit(solution)/shard_map/slice | solution.py:15
  73.5 5.7 %copy.216 = f32[15,2,1,512]{3,1,2,0:T(2,128)} copy(f32[15,2,1,512]{2,3,1,0:T(8,128)} %get-tuple-element.23) | data formatting | bytes 122880 | tf_op jit(solution)/shard_map/slice | solution.py:16
  89.1 5.7 %copy.219 = f32[15,2,32,512]{3,1,2,0:T(2,128)S(1)} copy(f32[15,2,32,512]{2,3,1,0:T(8,128)} %broadcast_multiply_fusion) | data formatting | bytes 3932160 | tf_op jit(solution)/shard_map/mul | solution.py:74
  94.8 5.6 %copy.213 = f32[15,2,1,512]{3,1,2,0:T(2,128)} copy(f32[15,2,1,512]{2,3,1,0:T(8,128)} %get-tuple-element.22) | data formatting | bytes 122880 | tf_op jit(solution)/shard_map/slice | solution.py:15
  117.7 5.7 %collective-permute-start.23 = (f32[15,2,10,1]{3,1,2,0:T(2,128)S(1)}, f32[15,2,10,1]{3,1,2,0:T(2,128)S(1)}, u32[]{:S(2)}, u32[]{:S(2)}) collective-permute-start(f32[15,2,10,1]{3,1,2,0:T(2,128)S(1)} %get-tuple-element.51), channel_id=1, source_target_pairs={{0,2},{2,4},{4,6},{1,3},{3,5},{5,7},{8,10},{10,12},{12,14},{9,11},... | collective-permute-start | bytes 3608 | tf_op jit(solution)/shard_map/ppermute | solution.py:19
  139.0 6.5 %collective-permute-start.27 = (f32[15,2,10,1]{3,1,2,0:T(2,128)}, f32[15,2,10,1]{3,1,2,0:T(2,128)}, u32[]{:S(2)}, u32[]{:S(2)}) collective-permute-start(f32[15,2,10,1]{3,1,2,0:T(2,128)} %get-tuple-element.47), channel_id=1, source_target_pairs={{0,2},{2,4},{4,6},{1,3},{3,5},{5,7},{8,10},{10,12},{12,14},{9,11},... | collective-permute-start | bytes 3608 | tf_op jit(solution)/shard_map/ppermute | solution.py:19
  153.1 7.2 %collective-permute-start.7 = (f32[15,2,34,1]{3,1,2,0:T(2,128)}, f32[15,2,34,1]{3,1,2,0:T(2,128)}, u32[]{:S(2)}, u32[]{:S(2)}) collective-permute-start(f32[15,2,34,1]{3,1,2,0:T(2,128)} %get-tuple-element.35), channel_id=1, source_target_pairs={{0,2},{2,4},{4,6},{1,3},{3,5},{5,7},{8,10},{10,12},{12,14},{9,11},... | collective-permute-start | bytes 12248 | tf_op jit(solution)/shard_map/ppermute | solution.py:19
  174.8 9.8 %pad_maximum_fusion.21 = (f32[15,2,32,512]{3,1,2,0:T(2,128)}, f32[15,2,32,512]{3,1,2,0:T(2,128)}) fusion(f32[15,2,34,1]{3,1,2,0:T(2,128)} %collective-permute-done.6, f32[15,2,1,512]{3,1,2,0:T(2,128)S(1)} %collective-permute-done.4, f32[15,2,32,512]{3,1,2,0:T(2,128)S(1)} %copy.219, f32[15,2,1,512]{3,1,2,0:T(2,128)S(1)} %collective-permute-done.5, ...), kind=kLoop, calls=%fused_computation.46 | loop fusion | flops 2949120 | bytes 6029280 | tf_op jit(solution)/shard_map/concatenate | solution.py:17
  184.6 6.3 %copy.258 = f32[15,2,32,512]{2,3,1,0:T(8,128)} copy(f32[15,2,32,512]{3,1,2,0:T(2,128)} %get-tuple-element.33) | data formatting | bytes 3932160
  195.9 22.4 %fusion.21 = f32[15,2,32,512]{2,3,1,0:T(8,128)} fusion(f32[15,2,32,512]{2,3,1,0:T(8,128)} %broadcast_multiply_fusion, f32[15,2,1,512]{2,3,1,0:T(8,128)} %copy.217, f32[15,2,1,512]{2,3,1,0:T(8,128)} %copy.214, f32[15,2,32,512]{2,3,1,0:T(8,128)} %copy.258, f32[15,2,32,512]{2,3,1,0:T(8,128)} %copy.257, f32[32,512]{0,1:T(8,128)S(1)} %copy.221, ...), kind=kLoop, calls=%fused_computation.26 | loop fusion | flops 6881280 | bytes 8249344 | tf_op jit(solution)/shard_map/add | solution.py:38
  218.3 13.0 %fusion.59 = (f32[15,2,1,512]{2,3,1,0:T(8,128)}, f32[15,2,1,512]{2,3,1,0:T(8,128)}) fusion(f32[15,2,32,512]{2,3,1,0:T(8,128)} %fusion.21), kind=kLoop, calls=%fused_computation.148 | loop fusion | bytes 245760 | tf_op jit(solution)/shard_map/slice | solution.py:15
  241.5 5.6 %copy.223 = f32[15,2,1,512]{3,1,2,0:T(2,128)} copy(f32[15,2,1,512]{2,3,1,0:T(8,128)} %get-tuple-element.20) | data formatting | bytes 122880 | tf_op jit(solution)/shard_map/slice | solution.py:15
  249.8 5.7 %copy.227 = f32[15,2,32,512]{3,1,2,0:T(2,128)S(1)} copy(f32[15,2,32,512]{2,3,1,0:T(8,128)} %fusion.21) | data formatting | bytes 3932160 | tf_op jit(solution)/shard_map/add | solution.py:38
  258.6 5.9 %collective-permute-start.11 = (f32[15,2,34,1]{3,1,2,0:T(2,128)}, f32[15,2,34,1]{3,1,2,0:T(2,128)}, u32[]{:S(2)}, u32[]{:S(2)}) collective-permute-start(f32[15,2,34,1]{3,1,2,0:T(2,128)} %get-tuple-element.31), channel_id=1, source_target_pairs={{0,2},{2,4},{4,6},{1,3},{3,5},{5,7},{8,10},{10,12},{12,14},{9,11},... | collective-permute-start | bytes 12248 | tf_op jit(solution)/shard_map/ppermute | solution.py:19
  281.4 9.8 %pad_maximum_fusion.15 = (f32[15,2,32,512]{3,1,2,0:T(2,128)}, f32[15,2,32,512]{3,1,2,0:T(2,128)}) fusion(f32[15,2,34,1]{3,1,2,0:T(2,128)} %collective-permute-done.10, f32[15,2,1,512]{3,1,2,0:T(2,128)S(1)} %collective-permute-done.8, f32[15,2,32,512]{3,1,2,0:T(2,128)S(1)} %copy.227, f32[15,2,1,512]{3,1,2,0:T(2,128)S(1)} %collective-permute-done.9, ...), kind=kLoop, calls=%fused_computation.40 | loop fusion | flops 2949120 | bytes 6029280 | tf_op jit(solution)/shard_map/concatenate | solution.py:17
  291.2 6.3 %copy.260 = f32[15,2,32,512]{2,3,1,0:T(8,128)} copy(f32[15,2,32,512]{3,1,2,0:T(2,128)} %get-tuple-element.29) | data formatting | bytes 3932160
  302.5 22.4 %fusion.14 = f32[15,2,32,512]{2,3,1,0:T(8,128)} fusion(f32[15,2,32,512]{2,3,1,0:T(8,128)} %fusion.21, f32[15,2,1,512]{2,3,1,0:T(8,128)} %copy.226, f32[15,2,1,512]{2,3,1,0:T(8,128)} %copy.224, f32[15,2,32,512]{2,3,1,0:T(8,128)} %copy.260, f32[15,2,32,512]{2,3,1,0:T(8,128)} %copy.259, f32[32,512]{0,1:T(8,128)S(1)} %copy.221, f32[32,512]{0,1:T(8,128)S(1)} %copy.218, ...), kind=kLoop, calls=%fused_computation.17 | loop fusion | flops 6881280 | bytes 8249344 | tf_op jit(solution)/shard_map/add | solution.py:38
  324.9 13.1 %fusion.58 = (f32[15,2,1,512]{2,3,1,0:T(8,128)}, f32[15,2,1,512]{2,3,1,0:T(8,128)}) fusion(f32[15,2,32,512]{2,3,1,0:T(8,128)} %fusion.14), kind=kLoop, calls=%fused_computation.147 | loop fusion | bytes 245760 | tf_op jit(solution)/shard_map/slice | solution.py:15
  338.0 5.6 %copy.232 = f32[15,2,1,512]{3,1,2,0:T(2,128)} copy(f32[15,2,1,512]{2,3,1,0:T(8,128)} %get-tuple-element.19) | data formatting | bytes 122880 | tf_op jit(solution)/shard_map/slice | solution.py:16
  357.2 5.7 %copy.234 = f32[15,2,32,512]{3,1,2,0:T(2,128)S(1)} copy(f32[15,2,32,512]{2,3,1,0:T(8,128)} %fusion.14) | data formatting | bytes 3932160 | tf_op jit(solution)/shard_map/add | solution.py:38
  366.0 5.8 %collective-permute-start.15 = (f32[15,2,34,1]{3,1,2,0:T(2,128)}, f32[15,2,34,1]{3,1,2,0:T(2,128)}, u32[]{:S(2)}, u32[]{:S(2)}) collective-permute-start(f32[15,2,34,1]{3,1,2,0:T(2,128)} %get-tuple-element.27), channel_id=1, source_target_pairs={{0,2},{2,4},{4,6},{1,3},{3,5},{5,7},{8,10},{10,12},{12,14},{9,11},... | collective-permute-start | bytes 12248 | tf_op jit(solution)/shard_map/ppermute | solution.py:19
  384.0 9.8 %pad_maximum_fusion.9 = (f32[15,2,32,512]{3,1,2,0:T(2,128)}, f32[15,2,32,512]{3,1,2,0:T(2,128)}) fusion(f32[15,2,34,1]{3,1,2,0:T(2,128)} %collective-permute-done.14, f32[15,2,1,512]{3,1,2,0:T(2,128)S(1)} %copy-done.9, f32[15,2,32,512]{3,1,2,0:T(2,128)S(1)} %copy.234, f32[15,2,1,512]{3,1,2,0:T(2,128)S(1)} %copy-done.7, ...), kind=kLoop, calls=%fused_computation.34 | loop fusion | flops 2949120 | bytes 6029280 | tf_op jit(solution)/shard_map/concatenate | solution.py:17
  393.8 6.3 %copy.262 = f32[15,2,32,512]{2,3,1,0:T(8,128)} copy(f32[15,2,32,512]{3,1,2,0:T(2,128)} %get-tuple-element.25) | data formatting | bytes 3932160
  400.1 6.1 %copy.261 = f32[15,2,32,512]{2,3,1,0:T(8,128)} copy(f32[15,2,32,512]{3,1,2,0:T(2,128)} %get-tuple-element.24) | data formatting | bytes 3932160
  410.7 25.6 %fusion.7 = f32[2,32,512]{1,2,0:T(8,128)S(1)} fusion(f32[15,2,32,512]{2,3,1,0:T(8,128)} %copy.255, f32[15,2,32,512]{2,3,1,0:T(8,128)} %bitcast.18, f32[15,2,32,512]{2,3,1,0:T(8,128)} %fusion.14, f32[15,2,1,512]{2,3,1,0:T(8,128)} %copy.233, f32[15,2,1,512]{2,3,1,0:T(8,128)} %copy.231, f32[15,2,32,512]{2,3,1,0:T(8,128)} %copy.262, ...), kind=kLoop, calls=%fused_computation.8 | loop fusion | flops 8323072 | bytes 10346496 | tf_op jit(solution)/shard_map/reduce_sum | solution.py:80
  437.9 19.3 %all-reduce.3.cloned.1.call-done = f32[2,32,512]{2,1,0:T(8,128)} async-done(((f32[2,32,512]{2,1,0:T(8,128)}), f32[2,32,512]{2,1,0:T(8,128)}) %all-reduce.3.cloned.1.call-update) | async-done | bytes 131088 | tf_op jit(solution)/shard_map/psum | solution.py:81
  458.7 42.6 %all-reduce = (f32[]{:T(128)}, f32[]{:T(128)}) all-reduce(f32[]{:T(128)} %multiply_reduce_fusion.2, f32[]{:T(128)} %get-tuple-element.16), channel_id=1, replica_groups=mesh['gx'=4,'gy'=4,'ma'=2] {'gx','gy'}, use_global_device_ids=true, to_apply=%region_1.0 | all-reduce | flops 2 | bytes 16 | tf_op jit(solution)/shard_map/psum | solution.py:82
  503.2 37.2 %psum.31 = f32[]{:T(128)} all-reduce(f32[]{:T(128)} %get-tuple-element.14), channel_id=1, replica_groups=mesh['gx'=4,'gy'=4,'ma'=2] {'gx','gy'}, use_global_device_ids=true, to_apply=%region_8.0 | all-reduce | flops 1 | bytes 8 | tf_op jit(solution)/shard_map/psum | solution.py:87
  (176 shorter events, 158.2 us)
Async XLA Ops:
  7.2 450.0 %all-reduce.3.cloned.1.call-start = ((), (), s32[]{:S(2)}) async-start(), calls=%async_computation | async-start | bytes 262144 | tf_op jit(solution)/shard_map/psum | solution.py:81
  47.6 68.5 %collective-permute-start.21 = (f32[15,2,1,128]{3,2,1,0:T(1,128)S(1)}, f32[15,2,1,128]{3,2,1,0:T(1,128)S(1)}, u32[]{:S(2)}, u32[]{:S(2)}) collective-permute-start(f32[15,2,1,128]{3,2,1,0:T(1,128)S(1)} %get-tuple-element.61), channel_id=1, source_target_pairs={{0,8},{8,16},{16,24},{1,9},{9,17},{17,25},{2,10},{10,18},{18,26},{... | collective-permute-start | bytes 46088 | tf_op jit(solution)/shard_map/ppermute | solution.py:19
  52.6 63.5 %collective-permute-start.20 = (f32[15,2,1,128]{3,2,1,0:T(1,128)S(1)}, f32[15,2,1,128]{3,2,1,0:T(1,128)S(1)}, u32[]{:S(2)}, u32[]{:S(2)}) collective-permute-start(f32[15,2,1,128]{3,2,1,0:T(1,128)S(1)} %get-tuple-element.60), channel_id=1, source_target_pairs={{8,0},{16,8},{24,16},{9,1},{17,9},{25,17},{10,2},{18,10},{26,18},{... | collective-permute-start | bytes 46088 | tf_op jit(solution)/shard_map/ppermute | solution.py:21
  53.9 29.2 %collective-permute-start.17 = (f32[2,3,128]{2,1,0:T(4,128)S(1)}, f32[2,3,128]{2,1,0:T(4,128)S(1)}, u32[]{:S(2)}, u32[]{:S(2)}) collective-permute-start(f32[2,3,128]{2,1,0:T(4,128)S(1)} %get-tuple-element.75), channel_id=1, source_target_pairs={{8,0},{16,8},{24,16},{9,1},{17,9},{25,17},{10,2},{18,10},{26,18},{... | collective-permute-start | bytes 9224 | tf_op jit(solution)/shard_map/ppermute | solution.py:21
  55.2 27.9 %collective-permute-start.16 = (f32[2,3,128]{2,1,0:T(4,128)S(1)}, f32[2,3,128]{2,1,0:T(4,128)S(1)}, u32[]{:S(2)}, u32[]{:S(2)}) collective-permute-start(f32[2,3,128]{2,1,0:T(4,128)S(1)} %get-tuple-element.74), channel_id=1, source_target_pairs={{0,8},{8,16},{16,24},{1,9},{9,17},{17,25},{2,10},{10,18},{18,26},{... | collective-permute-start | bytes 9224 | tf_op jit(solution)/shard_map/ppermute | solution.py:19
  79.2 70.9 %collective-permute-start.5 = (f32[15,2,1,512]{3,1,2,0:T(2,128)}, f32[15,2,1,512]{3,1,2,0:T(2,128)S(1)}, u32[]{:S(2)}, u32[]{:S(2)}) collective-permute-start(f32[15,2,1,512]{3,1,2,0:T(2,128)} %copy.216), channel_id=1, source_target_pairs={{0,8},{8,16},{16,24},{1,9},{9,17},{17,25},{2,10},{10,18},{18,26},{... | collective-permute-start | bytes 184328 | tf_op jit(solution)/shard_map/ppermute | solution.py:19
  83.2 17.2 %collective-permute-start.19 = (f32[2,14,3]{2,1,0:T(8,128)S(1)}, f32[2,14,3]{2,1,0:T(8,128)S(1)}, u32[]{:S(2)}, u32[]{:S(2)}) collective-permute-start(f32[2,14,3]{2,1,0:T(8,128)S(1)} %get-tuple-element.69), channel_id=1, source_target_pairs={{2,0},{4,2},{6,4},{3,1},{5,3},{7,5},{10,8},{12,10},{14,12},{11,9},... | collective-permute-start | bytes 1016 | tf_op jit(solution)/shard_map/ppermute | solution.py:21
  84.6 17.2 %collective-permute-start.18 = (f32[2,14,3]{2,1,0:T(8,128)S(1)}, f32[2,14,3]{2,1,0:T(8,128)S(1)}, u32[]{:S(2)}, u32[]{:S(2)}) collective-permute-start(f32[2,14,3]{2,1,0:T(8,128)S(1)} %get-tuple-element.68), channel_id=1, source_target_pairs={{0,2},{2,4},{4,6},{1,3},{3,5},{5,7},{8,10},{10,12},{12,14},{9,11},... | collective-permute-start | bytes 1016 | tf_op jit(solution)/shard_map/ppermute | solution.py:19
  100.5 6.2 %collective-permute-start.1 = (f32[2,3,512]{2,1,0:T(4,128)S(1)}, f32[2,3,512]{2,1,0:T(4,128)S(1)}, u32[]{:S(2)}, u32[]{:S(2)}) collective-permute-start(f32[2,3,512]{2,1,0:T(4,128)S(1)} %get-tuple-element.55), channel_id=1, source_target_pairs={{8,0},{16,8},{24,16},{9,1},{17,9},{25,17},{10,2},{18,10},{26,18},{... | collective-permute-start | bytes 36872 | tf_op jit(solution)/shard_map/ppermute | solution.py:21
  101.8 6.0 %collective-permute-start = (f32[2,3,512]{2,1,0:T(4,128)S(1)}, f32[2,3,512]{2,1,0:T(4,128)S(1)}, u32[]{:S(2)}, u32[]{:S(2)}) collective-permute-start(f32[2,3,512]{2,1,0:T(4,128)S(1)} %get-tuple-element.54), channel_id=1, source_target_pairs={{0,8},{8,16},{16,24},{1,9},{9,17},{17,25},{2,10},{10,18},{18,26},{... | collective-permute-start | bytes 36872 | tf_op jit(solution)/shard_map/ppermute | solution.py:19
  107.8 6.4 %collective-permute-start.3 = (f32[2,38,3]{2,1,0:T(8,128)S(1)}, f32[2,38,3]{2,1,0:T(8,128)S(1)}, u32[]{:S(2)}, u32[]{:S(2)}) collective-permute-start(f32[2,38,3]{2,1,0:T(8,128)S(1)} %get-tuple-element.39), channel_id=1, source_target_pairs={{2,0},{4,2},{6,4},{3,1},{5,3},{7,5},{10,8},{12,10},{14,12},{11,9},... | collective-permute-start | bytes 2744 | tf_op jit(solution)/shard_map/ppermute | solution.py:21
  109.1 6.6 %collective-permute-start.2 = (f32[2,38,3]{2,1,0:T(8,128)S(1)}, f32[2,38,3]{2,1,0:T(8,128)S(1)}, u32[]{:S(2)}, u32[]{:S(2)}) collective-permute-start(f32[2,38,3]{2,1,0:T(8,128)S(1)} %get-tuple-element.38), channel_id=1, source_target_pairs={{0,2},{2,4},{4,6},{1,3},{3,5},{5,7},{8,10},{10,12},{12,14},{9,11},... | collective-permute-start | bytes 2744 | tf_op jit(solution)/shard_map/ppermute | solution.py:19
  114.2 35.9 %collective-permute-start.4 = (f32[15,2,1,512]{3,1,2,0:T(2,128)}, f32[15,2,1,512]{3,1,2,0:T(2,128)S(1)}, u32[]{:S(2)}, u32[]{:S(2)}) collective-permute-start(f32[15,2,1,512]{3,1,2,0:T(2,128)} %copy.213), channel_id=1, source_target_pairs={{8,0},{16,8},{24,16},{9,1},{17,9},{25,17},{10,2},{18,10},{26,18},{... | collective-permute-start | bytes 184328 | tf_op jit(solution)/shard_map/ppermute | solution.py:21
  116.4 9.2 %collective-permute-start.22 = (f32[15,2,10,1]{3,1,2,0:T(2,128)S(1)}, f32[15,2,10,1]{3,1,2,0:T(2,128)S(1)}, u32[]{:S(2)}, u32[]{:S(2)}) collective-permute-start(f32[15,2,10,1]{3,1,2,0:T(2,128)S(1)} %get-tuple-element.50), channel_id=1, source_target_pairs={{2,0},{4,2},{6,4},{3,1},{5,3},{7,5},{10,8},{12,10},{14,12},{11,9},... | collective-permute-start | bytes 3608 | tf_op jit(solution)/shard_map/ppermute | solution.py:21
  117.7 8.4 %collective-permute-start.23 = (f32[15,2,10,1]{3,1,2,0:T(2,128)S(1)}, f32[15,2,10,1]{3,1,2,0:T(2,128)S(1)}, u32[]{:S(2)}, u32[]{:S(2)}) collective-permute-start(f32[15,2,10,1]{3,1,2,0:T(2,128)S(1)} %get-tuple-element.51), channel_id=1, source_target_pairs={{0,2},{2,4},{4,6},{1,3},{3,5},{5,7},{8,10},{10,12},{12,14},{9,11},... | collective-permute-start | bytes 3608 | tf_op jit(solution)/shard_map/ppermute | solution.py:19
  126.7 5.9 %collective-permute-start.25 = (f32[15,2,1,128]{3,2,1,0:T(1,128)S(1)}, f32[15,2,1,128]{3,2,1,0:T(1,128)S(1)}, u32[]{:S(2)}, u32[]{:S(2)}) collective-permute-start(f32[15,2,1,128]{3,2,1,0:T(1,128)S(1)} %get-tuple-element.59), channel_id=1, source_target_pairs={{0,8},{8,16},{16,24},{1,9},{9,17},{17,25},{2,10},{10,18},{18,26},{... | collective-permute-start | bytes 46088 | tf_op jit(solution)/shard_map/ppermute | solution.py:19
  137.7 8.7 %collective-permute-start.26 = (f32[15,2,10,1]{3,1,2,0:T(2,128)}, f32[15,2,10,1]{3,1,2,0:T(2,128)}, u32[]{:S(2)}, u32[]{:S(2)}) collective-permute-start(f32[15,2,10,1]{3,1,2,0:T(2,128)} %get-tuple-element.46), channel_id=1, source_target_pairs={{2,0},{4,2},{6,4},{3,1},{5,3},{7,5},{10,8},{12,10},{14,12},{11,9},... | collective-permute-start | bytes 3608 | tf_op jit(solution)/shard_map/ppermute | solution.py:21
  139.0 8.9 %collective-permute-start.27 = (f32[15,2,10,1]{3,1,2,0:T(2,128)}, f32[15,2,10,1]{3,1,2,0:T(2,128)}, u32[]{:S(2)}, u32[]{:S(2)}) collective-permute-start(f32[15,2,10,1]{3,1,2,0:T(2,128)} %get-tuple-element.47), channel_id=1, source_target_pairs={{0,2},{2,4},{4,6},{1,3},{3,5},{5,7},{8,10},{10,12},{12,14},{9,11},... | collective-permute-start | bytes 3608 | tf_op jit(solution)/shard_map/ppermute | solution.py:19
  151.9 22.9 %collective-permute-start.6 = (f32[15,2,34,1]{3,1,2,0:T(2,128)}, f32[15,2,34,1]{3,1,2,0:T(2,128)}, u32[]{:S(2)}, u32[]{:S(2)}) collective-permute-start(f32[15,2,34,1]{3,1,2,0:T(2,128)} %get-tuple-element.34), channel_id=1, source_target_pairs={{2,0},{4,2},{6,4},{3,1},{5,3},{7,5},{10,8},{12,10},{14,12},{11,9},... | collective-permute-start | bytes 12248 | tf_op jit(solution)/shard_map/ppermute | solution.py:21
  153.1 21.6 %collective-permute-start.7 = (f32[15,2,34,1]{3,1,2,0:T(2,128)}, f32[15,2,34,1]{3,1,2,0:T(2,128)}, u32[]{:S(2)}, u32[]{:S(2)}) collective-permute-start(f32[15,2,34,1]{3,1,2,0:T(2,128)} %get-tuple-element.35), channel_id=1, source_target_pairs={{0,2},{2,4},{4,6},{1,3},{3,5},{5,7},{8,10},{10,12},{12,14},{9,11},... | collective-permute-start | bytes 12248 | tf_op jit(solution)/shard_map/ppermute | solution.py:19
  160.5 87.9 %collective-permute-start.29 = (f32[15,2,1,128]{3,2,1,0:T(1,128)S(1)}, f32[15,2,1,128]{3,2,1,0:T(1,128)S(1)}, u32[]{:S(2)}, u32[]{:S(2)}) collective-permute-start(f32[15,2,1,128]{3,2,1,0:T(1,128)S(1)} %get-tuple-element.57), channel_id=1, source_target_pairs={{0,8},{8,16},{16,24},{1,9},{9,17},{17,25},{2,10},{10,18},{18,26},{... | collective-permute-start | bytes 46088 | tf_op jit(solution)/shard_map/ppermute | solution.py:19
  164.3 84.1 %collective-permute-start.28 = (f32[15,2,1,128]{3,2,1,0:T(1,128)S(1)}, f32[15,2,1,128]{3,2,1,0:T(1,128)S(1)}, u32[]{:S(2)}, u32[]{:S(2)}) collective-permute-start(f32[15,2,1,128]{3,2,1,0:T(1,128)S(1)} %get-tuple-element.56), channel_id=1, source_target_pairs={{8,0},{16,8},{24,16},{9,1},{17,9},{25,17},{10,2},{18,10},{26,18},{... | collective-permute-start | bytes 46088 | tf_op jit(solution)/shard_map/ppermute | solution.py:21
  236.9 18.6 %collective-permute-start.9 = (f32[15,2,1,512]{3,1,2,0:T(2,128)}, f32[15,2,1,512]{3,1,2,0:T(2,128)S(1)}, u32[]{:S(2)}, u32[]{:S(2)}) collective-permute-start(f32[15,2,1,512]{3,1,2,0:T(2,128)} %copy.225), channel_id=1, source_target_pairs={{0,8},{8,16},{16,24},{1,9},{9,17},{17,25},{2,10},{10,18},{18,26},{... | collective-permute-start | bytes 184328 | tf_op jit(solution)/shard_map/ppermute | solution.py:19
  247.1 8.4 %collective-permute-start.8 = (f32[15,2,1,512]{3,1,2,0:T(2,128)}, f32[15,2,1,512]{3,1,2,0:T(2,128)S(1)}, u32[]{:S(2)}, u32[]{:S(2)}) collective-permute-start(f32[15,2,1,512]{3,1,2,0:T(2,128)} %copy.223), channel_id=1, source_target_pairs={{8,0},{16,8},{24,16},{9,1},{17,9},{25,17},{10,2},{18,10},{26,18},{... | collective-permute-start | bytes 184328 | tf_op jit(solution)/shard_map/ppermute | solution.py:21
  257.3 24.1 %collective-permute-start.10 = (f32[15,2,34,1]{3,1,2,0:T(2,128)}, f32[15,2,34,1]{3,1,2,0:T(2,128)}, u32[]{:S(2)}, u32[]{:S(2)}) collective-permute-start(f32[15,2,34,1]{3,1,2,0:T(2,128)} %get-tuple-element.30), channel_id=1, source_target_pairs={{2,0},{4,2},{6,4},{3,1},{5,3},{7,5},{10,8},{12,10},{14,12},{11,9},... | collective-permute-start | bytes 12248 | tf_op jit(solution)/shard_map/ppermute | solution.py:21
  258.6 22.8 %collective-permute-start.11 = (f32[15,2,34,1]{3,1,2,0:T(2,128)}, f32[15,2,34,1]{3,1,2,0:T(2,128)}, u32[]{:S(2)}, u32[]{:S(2)}) collective-permute-start(f32[15,2,34,1]{3,1,2,0:T(2,128)} %get-tuple-element.31), channel_id=1, source_target_pairs={{0,2},{2,4},{4,6},{1,3},{3,5},{5,7},{8,10},{10,12},{12,14},{9,11},... | collective-permute-start | bytes 12248 | tf_op jit(solution)/shard_map/ppermute | solution.py:19
  265.4 89.7 %collective-permute-start.30 = (f32[15,2,10,1]{3,1,2,0:T(2,128)}, f32[15,2,10,1]{3,1,2,0:T(2,128)}, u32[]{:S(2)}, u32[]{:S(2)}) collective-permute-start(f32[15,2,10,1]{3,1,2,0:T(2,128)} %get-tuple-element.42), channel_id=1, source_target_pairs={{2,0},{4,2},{6,4},{3,1},{5,3},{7,5},{10,8},{12,10},{14,12},{11,9},... | collective-permute-start | bytes 3608 | tf_op jit(solution)/shard_map/ppermute | solution.py:21
  266.7 88.5 %collective-permute-start.31 = (f32[15,2,10,1]{3,1,2,0:T(2,128)}, f32[15,2,10,1]{3,1,2,0:T(2,128)}, u32[]{:S(2)}, u32[]{:S(2)}) collective-permute-start(f32[15,2,10,1]{3,1,2,0:T(2,128)} %get-tuple-element.43), channel_id=1, source_target_pairs={{0,2},{2,4},{4,6},{1,3},{3,5},{5,7},{8,10},{10,12},{12,14},{9,11},... | collective-permute-start | bytes 3608 | tf_op jit(solution)/shard_map/ppermute | solution.py:19
  343.7 19.3 %collective-permute-start.13 = (f32[15,2,1,512]{3,1,2,0:T(2,128)}, f32[15,2,1,512]{3,1,2,0:T(2,128)S(1)}, u32[]{:S(2)}, u32[]{:S(2)}) collective-permute-start(f32[15,2,1,512]{3,1,2,0:T(2,128)} %copy.232), channel_id=1, source_target_pairs={{0,8},{8,16},{16,24},{1,9},{9,17},{17,25},{2,10},{10,18},{18,26},{... | collective-permute-start | bytes 184328 | tf_op jit(solution)/shard_map/ppermute | solution.py:19
  353.9 9.1 %collective-permute-start.12 = (f32[15,2,1,512]{3,1,2,0:T(2,128)}, f32[15,2,1,512]{3,1,2,0:T(2,128)S(1)}, u32[]{:S(2)}, u32[]{:S(2)}) collective-permute-start(f32[15,2,1,512]{3,1,2,0:T(2,128)} %copy.230), channel_id=1, source_target_pairs={{8,0},{16,8},{24,16},{9,1},{17,9},{25,17},{10,2},{18,10},{26,18},{... | collective-permute-start | bytes 184328 | tf_op jit(solution)/shard_map/ppermute | solution.py:21
  364.8 19.3 %collective-permute-start.14 = (f32[15,2,34,1]{3,1,2,0:T(2,128)}, f32[15,2,34,1]{3,1,2,0:T(2,128)}, u32[]{:S(2)}, u32[]{:S(2)}) collective-permute-start(f32[15,2,34,1]{3,1,2,0:T(2,128)} %get-tuple-element.26), channel_id=1, source_target_pairs={{2,0},{4,2},{6,4},{3,1},{5,3},{7,5},{10,8},{12,10},{14,12},{11,9},... | collective-permute-start | bytes 12248 | tf_op jit(solution)/shard_map/ppermute | solution.py:21
  366.0 18.0 %collective-permute-start.15 = (f32[15,2,34,1]{3,1,2,0:T(2,128)}, f32[15,2,34,1]{3,1,2,0:T(2,128)}, u32[]{:S(2)}, u32[]{:S(2)}) collective-permute-start(f32[15,2,34,1]{3,1,2,0:T(2,128)} %get-tuple-element.27), channel_id=1, source_target_pairs={{0,2},{2,4},{4,6},{1,3},{3,5},{5,7},{8,10},{10,12},{12,14},{9,11},... | collective-permute-start | bytes 12248 | tf_op jit(solution)/shard_map/ppermute | solution.py:19
  (27 other events, 520.8 us)
Sparse Core Ops, SparseCore 0:
  437.4 19.7 all-reduce.2
where the time goes:
time: 561 us; the launch traced here: 550 us
  local copies, waits for them, and re-layouts  187 us (33%)
  other arithmetic  133 us (24%)
  starting transfers between devices  103 us (18%)
  blocking collectives  79.7 us (14%)
  waiting for transfers between devices  29.3 us (5%)
  between operations  18 us (3%)
    ppermute x16, starting transfers between devices, padded(): lax.ppermute(tail, axis, [(i, (i + 1) % count) for i in range(ends)])  82 us
    slice x12, local copies, waits for them, and re-layouts, padded(): head = lax.slice_in_dim(cells, 0, width, axis=dim)  58.2 us
    add x5, other arithmetic, stencil_pass(): return centre + along_x + along_y  45.8 us
    psum x1, blocking collectives, local(): norm_old = lax.psum(jnp.sum(residual * residual), ('gx', 'gy'))  42.6 us
    unnamed x60, local copies, waits for them, and re-layouts  41.9 us
    psum x1, blocking collectives, local(): norm_new = lax.psum(jnp.sum(new_residual * new_residual), ('gx', 'gy'))  37.2 us
    concatenate x12, other arithmetic, padded(): jnp.concatenate([lax.ppermute(tail, axis, [(i, (i + 1) % count) for i in...  34.4 us
    reduce_sum x1, other arithmetic, local(): partial_value = jnp.sum(perturbations * localized, axis=0) / (MEMBERS - 1)  25.6 us
  transfers between devices with their start and end apart: 33, of which 9 were waited for; matrix products, arithmetic and copies ran while one was open for 40% of the time, Pallas kernels for 0%

commit v1 on v0

v1 whole, which is shorter than its diff:
```python
import functools

import jax
import jax.numpy as jnp
from jax import lax
from jax.experimental import pallas as pl
from jax.experimental.pallas import tpu as pltpu
from jax.sharding import PartitionSpec as P

MEMBERS = 30
PASSES = 3
RATIO = 4
HALO = 4
LANES = 128
CHUNKS = 4
MESH = pl.DeviceIdType.MESH
F32 = jnp.float32
BF16 = jnp.bfloat16


def shift_up(u, axis):
    return pltpu.roll(u, u.shape[axis] - 1, axis)


def shift_down(u, axis):
    return pltpu.roll(u, 1, axis)


def split_dot(a, b):
    high = a.astype(BF16)
    low = (a - high.astype(F32)).astype(BF16)
    return jnp.dot(high, b, preferred_element_type=F32) + jnp.dot(
        low, b, preferred_element_type=F32
    )


def stencil_weights(cx, cy, rows, cols, has_prev, has_next, has_left, has_right):
    ext_rows, ext_cols = cx.shape
    row = lax.broadcasted_iota(jnp.int32, (ext_rows, ext_cols), 0)
    col = lax.broadcasted_iota(jnp.int32, (ext_rows, ext_cols), 1)
    outside = (
        ((row >= rows) & (row < rows + HALO) & (has_next == 0))
        | ((row >= rows + HALO) & (has_prev == 0))
        | ((col >= cols) & (col < cols + LANES // 2) & (has_right == 0))
        | ((col >= cols + LANES // 2) & (has_left == 0))
    )
    xp = 0.5 * (cx + shift_up(cx, 0))
    xm = shift_down(xp, 0)
    yp = 0.5 * (cy + shift_up(cy, 1))
    ym = shift_down(yp, 1)
    centre = 1.0 - xp - xm - yp - ym
    return [jnp.where(outside, 0.0, value) for value in (centre, xp, xm, yp, ym)]


def apply_passes(u, weights):
    for _ in range(PASSES):
        u = (
            weights[0][...] * u
            + weights[1][...] * shift_up(u, 0)
            + weights[2][...] * shift_down(u, 0)
            + weights[3][...] * shift_up(u, 1)
            + weights[4][...] * shift_down(u, 1)
        )
    return u


def kernel(
    sizes,
    p_ref, coef_ref, ccoef_ref, r_ref, d_ref,
    q_ref, sums_ref,
    wf, wc, line, lanes_out,
    x_top, x_bottom, c_top, c_bottom, strips,
    rx_next, rx_prev, rc_next, rc_prev, ry, rd,
    hy, hyc, fine_weights, coarse_weights,
    acc, acc_other, part, slots,
    send_sem, recv_sem, group_send, group_recv,
):
    n_x, n_y = sizes
    half, levels, rows, cols = p_ref.shape
    crows, ccols = ccoef_ref.shape[1], ccoef_ref.shape[2]
    gx, gy, ma = lax.axis_index("gx"), lax.axis_index("gy"), lax.axis_index("ma")
    me = gx * n_y + gy
    group = n_x * n_y
    has = {
        (-1, 0): gx > 0, (1, 0): gx < n_x - 1, (0, -1): gy > 0, (0, 1): gy < n_y - 1,
    }
    for dx in (-1, 1):
        for dy in (-1, 1):
            has[(dx, dy)] = has[(dx, 0)] & has[(0, dy)]

    barrier = pltpu.get_barrier_semaphore()

    def greet(k, carry):
        @pl.when(k != me)
        def _():
            pl.semaphore_signal(
                barrier, inc=1, device_id={"gx": k // n_y, "gy": k % n_y}, device_id_type=MESH
            )
        return carry

    lax.fori_loop(0, group, greet, 0)
    pl.semaphore_signal(barrier, inc=1, device_id={"ma": 1 - ma}, device_id_type=MESH)

    def zero_if(absent, ref):
        @pl.when(absent)
        def _():
            ref[...] = jnp.zeros_like(ref)

    zero_if(gx == 0, rx_prev)
    zero_if(gx == 0, rc_prev)
    zero_if(gx == n_x - 1, rx_next)
    zero_if(gx == n_x - 1, rc_next)
    for side in (0, 1):
        dy = 2 * side - 1
        zero_if(jnp.logical_not(has[(0, dy)]), ry.at[side])
        for way in (0, 1):
            zero_if(jnp.logical_not(has[(2 * way - 1, dy)]), rd.at[side, way])

    def weigh(m, carry):
        w = p_ref[m] * d_ref[...]
        wf[m] = w
        x_top[m] = w[:, :HALO]
        x_bottom[m] = w[:, rows - HALO :]
        return carry

    coefs = coef_ref[...]
    wf[half] = coefs
    x_top[half] = coefs[:, :HALO]
    x_bottom[half] = coefs[:, rows - HALO :]
    lax.fori_loop(0, half, weigh, 0)

    pl.semaphore_wait(barrier, group)

    moves = []

    def move(src, dst, dx, dy):
        slot = len(moves)
        target = {
            "gx": jnp.clip(gx + dx, 0, n_x - 1) if dx else gx,
            "gy": jnp.clip(gy + dy, 0, n_y - 1) if dy else gy,
        }
        copy = pltpu.make_async_remote_copy(
            src_ref=src, dst_ref=dst, send_sem=send_sem.at[slot], recv_sem=recv_sem.at[slot],
            device_id=target, device_id_type=MESH,
        )
        moves.append((copy, has[(dx, dy)], has[(-dx, -dy)]))

        @pl.when(has[(dx, dy)])
        def _():
            copy.start()

        return slot

    def arrive(slot):
        @pl.when(moves[slot][2])
        def _():
            moves[slot][0].wait_recv()

    total = half + 1
    bounds = [total - (total * k) // CHUNKS for k in range(CHUNKS + 1)]
    x_moves = []
    for k in range(CHUNKS):
        low, high = bounds[k + 1], bounds[k]
        span = pl.ds(low, high - low)
        x_moves.append(
            (
                move(x_top.at[span], rx_next.at[span], -1, 0),
                move(x_bottom.at[span], rx_prev.at[span], 1, 0),
                low, high,
            )
        )

    pick = lax.broadcasted_iota(jnp.int32, (cols, ccols), 0) // RATIO
    gather = jnp.where(
        pick == lax.broadcasted_iota(jnp.int32, (cols, ccols), 1), 1.0 / RATIO**2, 0.0
    ).astype(BF16)

    def restrict(m, carry):
        values = wf[m].reshape(levels * rows, cols)
        line[pl.ds(pl.multiple_of(m * levels * rows, 8), levels * rows)] = split_dot(values, gather)
        return carry

    lax.fori_loop(0, half, restrict, 0)
    count = half * levels * crows
    coarse = line[pl.ds(0, count, stride=RATIO), :]
    for k in range(1, RATIO):
        coarse = coarse + line[pl.ds(k, count, stride=RATIO), :]
    wc[pl.ds(0, half)] = coarse.reshape(half, levels, crows, ccols)
    wc[half] = ccoef_ref[...]
    every = wc[...]
    c_top[...] = every[:, :, :HALO]
    c_bottom[...] = every[:, :, crows - HALO :]
    c_moves = [move(c_top, rc_next, -1, 0), move(c_bottom, rc_prev, 1, 0)]

    flane = lax.broadcasted_iota(jnp.int32, (rows, LANES), 1)
    clane = lax.broadcasted_iota(jnp.int32, (crows, LANES), 1)

    def pack(m, carry):
        fl, fr, cl, cr = carry
        for level in range(levels):
            at = PASSES * (m * levels + level)
            fmask = (flane >= at) & (flane < at + PASSES)
            cmask = (clane >= at) & (clane < at + PASSES)
            fl = jnp.where(fmask, pltpu.roll(wf[m, level, :, :LANES], at, 1), fl)
            fr = jnp.where(fmask, pltpu.roll(wf[m, level, :, cols - LANES :], at + PASSES, 1), fr)
            field = wc[m, level]
            cl = jnp.where(cmask, pltpu.roll(field[:, :LANES], at, 1), cl)
            cr = jnp.where(cmask, pltpu.roll(field[:, ccols - LANES :], at + PASSES, 1), cr)
        return fl, fr, cl, cr

    fzero = jnp.zeros((rows, LANES), F32)
    czero = jnp.zeros((crows, LANES), F32)
    fl, fr, cl, cr = lax.fori_loop(0, total, pack, (fzero, fzero, czero, czero))
    for side, (fine, small) in enumerate(((fl, cl), (fr, cr))):
        strips[side, 0:crows] = small
        strips[side, crows : crows + rows] = fine
        strips[side, crows + rows :] = small
    y_moves = []
    for side in (0, 1):
        dy = 2 * side - 1
        other = 1 - side
        y_moves.append(move(strips.at[side, pl.ds(0, crows + rows)], ry.at[other], 0, dy))
        y_moves.append(move(strips.at[side, pl.ds(0, 16)], rd.at[other, 1], -1, dy))
        y_moves.append(move(strips.at[side, pl.ds(crows + rows - 8, 16)], rd.at[other, 0], 1, dy))

    for slot in y_moves:
        arrive(slot)
    for slot in c_moves:
        arrive(slot)

    near = lax.broadcasted_iota(jnp.int32, (8, LANES), 0) < HALO
    for side in (0, 1):
        hyc[side, 0:crows] = ry[side, 0:crows]
        hyc[side, crows : crows + 8] = jnp.where(near, rd[side, 1, 0:8], rd[side, 0, 8:16])
        hy[side, 0:rows] = ry[side, crows : crows + rows]
        hy[side, rows : rows + 8] = jnp.where(near, rd[side, 1, 8:16], rd[side, 0, 0:8])

    def columns(ref, index, height):
        lane = lax.broadcasted_iota(jnp.int32, (height, LANES), 1)
        at = PASSES * index
        right = pltpu.roll(ref[1], LANES - at, 1)
        left = pltpu.roll(ref[0], LANES - PASSES - at, 1)
        return jnp.where(
            lane < PASSES, right, jnp.where(lane >= LANES - PASSES, left, 0.0)
        )

    def extended(main, nxt, prv, ref, index):
        height = main.shape[0] + 2 * HALO
        tall = jnp.concatenate([main, jnp.concatenate([nxt, prv], axis=0)], axis=0)
        return jnp.concatenate([tall, columns(ref, index, height)], axis=1)

    def coarse_field(m, level):
        return extended(
            wc[m, level], rc_next[m, level], rc_prev[m, level], hyc, m * levels + level
        )

    def fine_field(m, level):
        return extended(
            wf[m, level], rx_next[m, level], rx_prev[m, level], hy, m * levels + level
        )

    ends = [
        value.astype(jnp.int32)
        for value in (has[(-1, 0)], has[(1, 0)], has[(0, -1)], has[(0, 1)])
    ]
    for k, value in enumerate(
        stencil_weights(coarse_field(half, 0), coarse_field(half, 1), crows, ccols, *ends)
    ):
        coarse_weights[k] = value

    spread = jnp.where(
        lax.broadcasted_iota(jnp.int32, (ccols, cols), 1) // RATIO
        == lax.broadcasted_iota(jnp.int32, (ccols, cols), 0),
        1.0, 0.0,
    ).astype(BF16)

    def coarse_member(m, carry):
        for level in range(levels):
            u = apply_passes(coarse_field(m, level), [coarse_weights.at[k] for k in range(5)])
            start = pl.multiple_of((m * levels + level) * crows, 8)
            wc[m, level] = u[:crows, :ccols]
        return carry

    lax.fori_loop(0, half, coarse_member, 0)
    lanes_out[...] = split_dot(
        wc[pl.ds(0, half)].reshape(half * levels * crows, ccols), spread
    )

    acc[...] = jnp.zeros_like(acc)
    upper = lax.broadcasted_iota(jnp.int32, (2 * RATIO, cols), 0) < RATIO

    def fine_member(m, carry):
        for level in range(levels):
            u = apply_passes(fine_field(m, level), [fine_weights.at[k] for k in range(5)])
            u = u[:rows, :cols]
            base = (m * levels + level) * crows
            for t in range(rows // (2 * RATIO)):
                a = jnp.broadcast_to(lanes_out[pl.ds(base + 2 * t, 1), :], (2 * RATIO, cols))
                b = jnp.broadcast_to(lanes_out[pl.ds(base + 2 * t + 1, 1), :], (2 * RATIO, cols))
                at = slice(2 * RATIO * t, 2 * RATIO * (t + 1))
                acc[level, at] += p_ref[m, level, at] * (u[at] + jnp.where(upper, a, b))
        return carry

    for k, (first, second, low, high) in enumerate(x_moves):
        arrive(first)
        arrive(second)
        if k == 0:
            for j, value in enumerate(
                stencil_weights(fine_field(half, 0), fine_field(half, 1), rows, cols, *ends)
            ):
                fine_weights[j] = value
        lax.fori_loop(low, min(high, half), fine_member, 0)

    swap = pltpu.make_async_remote_copy(
        src_ref=acc, dst_ref=acc_other, send_sem=send_sem.at[len(moves)],
        recv_sem=recv_sem.at[len(moves)], device_id={"ma": 1 - ma}, device_id_type=MESH,
    )
    swap.start()
    swap.wait_recv()
    d, r = d_ref[...], r_ref[...]
    q = d + (acc[...] + acc_other[...]) / (MEMBERS - 1)
    q_ref[...] = q

    def total_row(value):
        flat = value.reshape(levels * rows // 8, 8, cols)
        tile = jnp.sum(flat, axis=0)
        narrow = tile[:, :LANES]
        for k in range(1, cols // LANES):
            narrow = narrow + tile[:, k * LANES : (k + 1) * LANES]
        return jnp.sum(narrow, axis=0, keepdims=True)

    row = lax.broadcasted_iota(jnp.int32, (8, LANES), 0)
    packed = jnp.zeros((8, LANES), F32)
    for k, value in enumerate((r * r, d * q, r * q, q * q)):
        packed = jnp.where(row == k, total_row(value), packed)
    part[...] = packed
    slots[me] = packed

    def to_peer(k):
        return pltpu.make_async_remote_copy(
            src_ref=part, dst_ref=slots.at[me], send_sem=group_send.at[k],
            recv_sem=group_recv.at[me],
            device_id={"gx": k // n_y, "gy": k % n_y}, device_id_type=MESH,
        )

    def from_peer(k):
        return pltpu.make_async_remote_copy(
            src_ref=part, dst_ref=slots.at[k], send_sem=group_send.at[k],
            recv_sem=group_recv.at[k],
            device_id={"gx": k // n_y, "gy": k % n_y}, device_id_type=MESH,
        )

    def each_peer(action):
        def body(k, carry):
            @pl.when(k != me)
            def _():
                action(k)
            return carry

        lax.fori_loop(0, group, body, 0)

    each_peer(lambda k: to_peer(k).start())
    each_peer(lambda k: from_peer(k).wait_recv())
    summed = jnp.sum(slots[...], axis=0)
    sums_ref[...] = jnp.broadcast_to(jnp.sum(summed, axis=1, keepdims=True), (8, LANES))

    each_peer(lambda k: to_peer(k).wait_send())
    swap.wait_send()
    for copy, sends, _ in moves:
        @pl.when(sends)
        def _():
            copy.wait_send()


def local(n_x, n_y, perturbations, coefficients, coarse_coefficients, iterate, residual, direction):
    half, levels, rows, cols = perturbations.shape
    _, crows, ccols = coarse_coefficients.shape
    total = half + 1
    group = n_x * n_y
    n_moves = 2 * CHUNKS + 2 + 6 + 1
    vmem = pl.BlockSpec(memory_space=pltpu.VMEM)
    q, sums = pl.pallas_call(
        functools.partial(kernel, (n_x, n_y)),
        out_shape=(
            jax.ShapeDtypeStruct((levels, rows, cols), F32),
            jax.ShapeDtypeStruct((8, LANES), F32),
        ),
        in_specs=[vmem] * 5,
        out_specs=(vmem, vmem),
        scratch_shapes=[
            pltpu.VMEM((total, levels, rows, cols), F32),
            pltpu.VMEM((total, levels, crows, ccols), F32),
            pltpu.VMEM((half * levels * rows, ccols), F32),
            pltpu.VMEM((half * levels * crows, cols), F32),
            pltpu.VMEM((total, levels, HALO, cols), F32),
            pltpu.VMEM((total, levels, HALO, cols), F32),
            pltpu.VMEM((total, levels, HALO, ccols), F32),
            pltpu.VMEM((total, levels, HALO, ccols), F32),
            pltpu.VMEM((2, rows + 2 * crows, LANES), F32),
            pltpu.VMEM((total, levels, HALO, cols), F32),
            pltpu.VMEM((total, levels, HALO, cols), F32),
            pltpu.VMEM((total, levels, HALO, ccols), F32),
            pltpu.VMEM((total, levels, HALO, ccols), F32),
            pltpu.VMEM((2, rows + crows, LANES), F32),
            pltpu.VMEM((2, 2, 16, LANES), F32),
            pltpu.VMEM((2, rows + 2 * HALO, LANES), F32),
            pltpu.VMEM((2, crows + 2 * HALO, LANES), F32),
            pltpu.VMEM((5, rows + 2 * HALO, cols + LANES), F32),
            pltpu.VMEM((5, crows + 2 * HALO, ccols + LANES), F32),
            pltpu.VMEM((levels, rows, cols), F32),
            pltpu.VMEM((levels, rows, cols), F32),
            pltpu.VMEM((8, LANES), F32),
            pltpu.VMEM((group, 8, LANES), F32),
            pltpu.SemaphoreType.DMA((n_moves,)),
            pltpu.SemaphoreType.DMA((n_moves,)),
            pltpu.SemaphoreType.DMA((group,)),
            pltpu.SemaphoreType.DMA((group,)),
        ],
        compiler_params=pltpu.CompilerParams(
            collective_id=0, has_side_effects=True, vmem_limit_bytes=48 << 20
        ),
    )(perturbations, coefficients, coarse_coefficients, residual, direction)
    norm_old, curvature, cross, image = (sums[k, 0] for k in range(4))
    step_length = norm_old / curvature
    norm_new = norm_old + step_length * (step_length * image - 2.0 * cross)
    new_iterate = iterate + step_length * direction
    new_residual = residual - step_length * q
    new_direction = new_residual + norm_new / norm_old * direction
    return (new_iterate, new_residual, new_direction)


def solution(mesh):
    cell = P(None, "gx", "gy")
    return jax.shard_map(
        functools.partial(local, mesh.shape["gx"], mesh.shape["gy"]),
        mesh=mesh,
        in_specs=(P("ma", None, "gx", "gy"), cell, cell, cell, cell, cell),
        out_specs=(cell, cell, cell),
        check_vma=False,
    )
```

time: 561 us -> 45.7 us (0.08); the launches traced: 550 us -> 45.4 us
  local copies, waits for them, and re-layouts: 187 us -> 5.51 us
  other arithmetic: 133 us -> 0.78 us
  starting transfers between devices: 103 us -> 0 us
  blocking collectives: 79.7 us -> 0 us
  Pallas kernels: 0 us -> 34.5 us
  waiting for transfers between devices: 29.3 us -> 0 us
  between operations: 18 us -> 4.61 us
    ppermute x32 -> x0, starting transfers between devices: 103 us -> none  [the longest x16 82 us: padded(): lax.ppermute(tail, axis, [(i, (i + 1) % count) for i in range(ends)])]
    psum x2 -> x0, blocking collectives: 79.7 us -> none  [the longest x1 42.6 us: local(): norm_old = lax.psum(jnp.sum(residual * residual), ('gx', 'gy'))]
    slice x25 -> x1, local copies, waits for them, and re-layouts: 75.9 us -> 0.55 us  [local(): norm_old, curvature, cross, image = (sums[k, 0] for k in range(4))]
    add x5 -> x0, other arithmetic: 45.8 us -> none  [stencil_pass(): return centre + along_x + along_y]
    reduce_sum x5 -> x0, other arithmetic: 38.5 us -> none  [the longest x1 25.6 us: local(): partial_value = jnp.sum(perturbations * localized, axis=0) / (MEMBERS - 1)]
    unnamed x60 -> x16, local copies, waits for them, and re-layouts: 41.9 us -> 4.96 us
    pallas_call x0 -> x1, Pallas kernels: none -> 34.5 us  [local(): pl.pallas_call(functools.partial(kernel, (n_x, n_y)), out_shape=(jax.Shap...]
    concatenate x12 -> x0, other arithmetic: 34.4 us -> none  [padded(): jnp.concatenate([lax.ppermute(tail, axis, [(i, (i + 1) % count) for i in...]
  transfers between devices with their start and end apart: 33 -> 0, of which waited for: 9 -> 0; matrix products, arithmetic and copies ran while one was open for 40% -> 0% of each run, Pallas kernels for 0% -> 0%
where the time goes in v1:
time: 45.7 us; the launch traced here: 45.4 us
  Pallas kernels  34.5 us (75%)
  local copies, waits for them, and re-layouts  5.51 us (12%)
  between operations  4.61 us (10%)
  other arithmetic  0.78 us (2%)
    pallas_call x1, Pallas kernels, local(): pl.pallas_call(functools.partial(kernel, (n_x, n_y)), out_shape=(jax.Shap...  34.5 us
    unnamed x16, local copies, waits for them, and re-layouts  4.96 us

profile of v1, /device:TPU:0, one launch (start us, length us, event | category | flops | bytes accessed | tf_op | source)
XLA Modules:
  0.0 45.4 jit_solution(8587136392436313025)
XLA Ops:
  0.6 0.0 copy-start
  0.6 1.5 %copy-done = f32[15,2,32,512]{3,2,1,0:T(8,128)S(1)} copy-done((f32[15,2,32,512]{3,2,1,0:T(8,128)S(1)}, f32[15,2,32,512]{3,2,1,0:T(8,128)}, u32[]{:S(2)}) %copy-start) | copy-done | bytes 1966104
  2.2 0.0 copy-start.1
  2.2 0.9 %copy-done.1 = f32[2,32,512]{2,1,0:T(8,128)S(1)} copy-done((f32[2,32,512]{2,1,0:T(8,128)S(1)}, f32[2,32,512]{2,1,0:T(8,128)}, u32[]{:S(2)}) %copy-start.1) | copy-done | bytes 131096
  3.1 0.0 copy-start.3
  3.1 0.9 %copy-done.3 = f32[2,32,512]{2,1,0:T(8,128)S(1)} copy-done((f32[2,32,512]{2,1,0:T(8,128)S(1)}, f32[2,32,512]{2,1,0:T(8,128)}, u32[]{:S(2)}) %copy-start.3) | copy-done | bytes 131096
  4.0 0.0 copy-start.5
  4.0 0.9 %copy-done.5 = f32[2,32,512]{2,1,0:T(8,128)S(1)} copy-done((f32[2,32,512]{2,1,0:T(8,128)S(1)}, f32[2,32,512]{2,1,0:T(8,128)}, u32[]{:S(2)}) %copy-start.5) | copy-done | bytes 131096
  4.9 0.0 copy-start.6
  4.9 0.7 %copy-done.6 = f32[2,8,128]{2,1,0:T(8,128)S(1)} copy-done((f32[2,8,128]{2,1,0:T(8,128)S(1)}, f32[2,8,128]{2,1,0:T(8,128)}, u32[]{:S(2)}) %copy-start.6) | copy-done | bytes 8216
  5.6 0.0 copy-start.2
  5.6 0.0 copy-start.4
  5.6 0.0 copy-start.7
  5.6 34.5 %shard_map.85 = (f32[2,32,512]{2,1,0:T(8,128)S(1)}, f32[8,128]{1,0:T(8,128)S(1)}) custom-call(f32[15,2,32,512]{3,2,1,0:T(8,128)S(1)} %copy-done, f32[2,32,512]{2,1,0:T(8,128)S(1)} %copy-done.5, f32[2,8,128]{2,1,0:T(8,128)S(1)} %copy-done.6, f32[2,32,512]{2,1,0:T(8,128)S(1)} %copy-done.3, f32[2,32,512]{2,1,0:T(8,128)S(1)} %copy-done.1), custom_call_target="tpu_custom_call" | custom-call | tf_op jit(solution)/shard_map/pallas_call | solution.py:382
  40.2 0.6 %fusion = (f32[1,1]{1,0:T(1,128)}, f32[1,1]{1,0:T(1,128)}, f32[1,1]{1,0:T(1,128)}, f32[1,1]{1,0:T(1,128)}) fusion(f32[8,128]{1,0:T(8,128)S(1)} %get-tuple-element.5), kind=kLoop, calls=%fused_computation.3 | loop fusion | bytes 32 | tf_op jit(solution)/shard_map/slice | solution.py:423
  44.6 0.0 copy-done.2
  44.6 0.0 copy-done.4
  44.7 0.0 copy-done.7
  44.7 0.8 %multiply_add_fusion = (f32[2,32,512]{2,1,0:T(8,128)}, f32[2,32,512]{2,1,0:T(8,128)}, f32[2,32,512]{2,1,0:T(8,128)}) fusion(f32[2,32,512]{2,1,0:T(8,128)S(1)} %copy-done.2, f32[]{:T(128)S(6)} %div.7, f32[2,32,512]{2,1,0:T(8,128)S(1)} %copy-done.4, f32[2,32,512]{2,1,0:T(8,128)S(1)} %get-tuple-element.6, f32[]{:T(128)S(6)} %div.6, f32[2,32,512]{2,1,0:T(8,128)S(1)} %copy-done.7), kind=kLoop, calls=%fused_computation | loop fusion | flops 196608 | bytes 917512 | tf_op jit(solution)/shard_map/add | solution.py:428
Async XLA Ops:
  0.6 1.5 %copy-start = (f32[15,2,32,512]{3,2,1,0:T(8,128)S(1)}, f32[15,2,32,512]{3,2,1,0:T(8,128)}, u32[]{:S(2)}) copy-start(f32[15,2,32,512]{3,2,1,0:T(8,128)} %p_ref.1) | copy-start | bytes 5898244
  2.2 0.9 %copy-start.1 = (f32[2,32,512]{2,1,0:T(8,128)S(1)}, f32[2,32,512]{2,1,0:T(8,128)}, u32[]{:S(2)}) copy-start(f32[2,32,512]{2,1,0:T(8,128)} %d_ref.1) | copy-start | bytes 393220
  3.1 0.9 %copy-start.3 = (f32[2,32,512]{2,1,0:T(8,128)S(1)}, f32[2,32,512]{2,1,0:T(8,128)}, u32[]{:S(2)}) copy-start(f32[2,32,512]{2,1,0:T(8,128)} %r_ref.1) | copy-start | bytes 393220
  4.0 0.9 %copy-start.5 = (f32[2,32,512]{2,1,0:T(8,128)S(1)}, f32[2,32,512]{2,1,0:T(8,128)}, u32[]{:S(2)}) copy-start(f32[2,32,512]{2,1,0:T(8,128)} %coef_ref.1) | copy-start | bytes 393220
  4.9 0.7 %copy-start.6 = (f32[2,8,128]{2,1,0:T(8,128)S(1)}, f32[2,8,128]{2,1,0:T(8,128)}, u32[]{:S(2)}) copy-start(f32[2,8,128]{2,1,0:T(8,128)} %ccoef_ref.1) | copy-start | bytes 24580
  5.6 39.0 %copy-start.2 = (f32[2,32,512]{2,1,0:T(8,128)S(1)}, f32[2,32,512]{2,1,0:T(8,128)}, u32[]{:S(2)}) copy-start(f32[2,32,512]{2,1,0:T(8,128)} %d_ref.1) | copy-start | bytes 393220
  5.6 39.1 %copy-start.4 = (f32[2,32,512]{2,1,0:T(8,128)S(1)}, f32[2,32,512]{2,1,0:T(8,128)}, u32[]{:S(2)}) copy-start(f32[2,32,512]{2,1,0:T(8,128)} %r_ref.1) | copy-start | bytes 393220
  5.6 39.1 %copy-start.7 = (f32[2,32,512]{2,1,0:T(8,128)S(1)}, f32[2,32,512]{2,1,0:T(8,128)}, u32[]{:S(2)}) copy-start(f32[2,32,512]{2,1,0:T(8,128)} %param.9) | copy-start | bytes 393220

commit v2 on v1

--- a/solution.py
+++ b/solution.py
@@ -66,14 +66,15 @@
 
 def kernel(
     sizes,
+    p_hbm, coef_hbm, ccoef_hbm, r_hbm, d_hbm,
+    q_ref, step_ref, growth_ref,
     p_ref, coef_ref, ccoef_ref, r_ref, d_ref,
-    q_ref, sums_ref,
-    wf, wc, line, lanes_out,
+    wc, line, lanes_out,
     x_top, x_bottom, c_top, c_bottom, strips,
     rx_next, rx_prev, rc_next, rc_prev, ry, rd,
     hy, hyc, fine_weights, coarse_weights,
     acc, acc_other, part, slots,
-    send_sem, recv_sem, group_send, group_recv,
+    load_sem, send_sem, recv_sem, group_send, group_recv,
 ):
     n_x, n_y = sizes
     half, levels, rows, cols = p_ref.shape
@@ -88,18 +89,36 @@
         for dy in (-1, 1):
             has[(dx, dy)] = has[(dx, 0)] & has[(0, dy)]
 
+    def each_peer(action):
+        def body(step, carry):
+            action(lax.rem(me + step, group))
+            return carry
+
+        lax.fori_loop(1, group, body, 0, unroll=group <= 16)
+
     barrier = pltpu.get_barrier_semaphore()
-
-    def greet(k, carry):
-        @pl.when(k != me)
-        def _():
-            pl.semaphore_signal(
-                barrier, inc=1, device_id={"gx": k // n_y, "gy": k % n_y}, device_id_type=MESH
-            )
-        return carry
-
-    lax.fori_loop(0, group, greet, 0)
     pl.semaphore_signal(barrier, inc=1, device_id={"ma": 1 - ma}, device_id_type=MESH)
+    each_peer(
+        lambda k: pl.semaphore_signal(
+            barrier, inc=1, device_id={"gx": k // n_y, "gy": k % n_y}, device_id_type=MESH
+        )
+    )
+
+    total = half + 1
+    bounds = [total - (total * k) // CHUNKS for k in range(CHUNKS + 1)]
+    loads = [
+        pltpu.make_async_copy(src, dst, load_sem.at[k])
+        for k, (src, dst) in enumerate(
+            ((d_hbm, d_ref), (coef_hbm, coef_ref), (ccoef_hbm, ccoef_ref), (r_hbm, r_ref))
+        )
+    ]
+    for k in range(CHUNKS):
+        span = pl.ds(bounds[k + 1], min(bounds[k], half) - bounds[k + 1])
+        loads.append(
+            pltpu.make_async_copy(p_hbm.at[span], p_ref.at[span], load_sem.at[4 + k])
+        )
+    for k in (0, 1, 4, 5, 6, 7, 2, 3):
+        loads[k].start()
 
     def zero_if(absent, ref):
         @pl.when(absent)
@@ -116,21 +135,6 @@
         for way in (0, 1):
             zero_if(jnp.logical_not(has[(2 * way - 1, dy)]), rd.at[side, way])
 
-    def weigh(m, carry):
-        w = p_ref[m] * d_ref[...]
-        wf[m] = w
-        x_top[m] = w[:, :HALO]
-        x_bottom[m] = w[:, rows - HALO :]
-        return carry
-
-    coefs = coef_ref[...]
-    wf[half] = coefs
-    x_top[half] = coefs[:, :HALO]
-    x_bottom[half] = coefs[:, rows - HALO :]
-    lax.fori_loop(0, half, weigh, 0)
-
-    pl.semaphore_wait(barrier, group)
-
     moves = []
 
     def move(src, dst, dx, dy):
@@ -156,11 +160,19 @@
         def _():
             moves[slot][0].wait_recv()
 
-    total = half + 1
-    bounds = [total - (total * k) // CHUNKS for k in range(CHUNKS + 1)]
+    loads[0].wait()
+    loads[1].wait()
+    x_top[half] = coef_ref[:, :HALO]
+    x_bottom[half] = coef_ref[:, rows - HALO :]
     x_moves = []
     for k in range(CHUNKS):
         low, high = bounds[k + 1], bounds[k]
+        loads[4 + k].wait()
+        for m in range(low, min(high, half)):
+            x_top[m] = p_ref[m, :, :HALO] * d_ref[:, :HALO]
+            x_bottom[m] = p_ref[m, :, rows - HALO :] * d_ref[:, rows - HALO :]
+        if k == 0:
+            pl.semaphore_wait(barrier, group)
         span = pl.ds(low, high - low)
         x_moves.append(
             (
@@ -174,43 +186,46 @@
     gather = jnp.where(
         pick == lax.broadcasted_iota(jnp.int32, (cols, ccols), 1), 1.0 / RATIO**2, 0.0
     ).astype(BF16)
-
-    def restrict(m, carry):
-        values = wf[m].reshape(levels * rows, cols)
-        line[pl.ds(pl.multiple_of(m * levels * rows, 8), levels * rows)] = split_dot(values, gather)
+    batch = next(k for k in (5, 3, 2, 1) if half % k == 0)
+
+    def restrict(j, carry):
+        tall = batch * levels * rows
+        values = (p_ref[pl.ds(j * batch, batch)] * d_ref[...][None]).reshape(tall, cols)
+        line[pl.ds(pl.multiple_of(j * tall, 8), tall)] = split_dot(values, gather)
         return carry
 
-    lax.fori_loop(0, half, restrict, 0)
+    lax.fori_loop(0, half // batch, restrict, 0)
     count = half * levels * crows
     coarse = line[pl.ds(0, count, stride=RATIO), :]
     for k in range(1, RATIO):
         coarse = coarse + line[pl.ds(k, count, stride=RATIO), :]
+    loads[2].wait()
     wc[pl.ds(0, half)] = coarse.reshape(half, levels, crows, ccols)
     wc[half] = ccoef_ref[...]
-    every = wc[...]
-    c_top[...] = every[:, :, :HALO]
-    c_bottom[...] = every[:, :, crows - HALO :]
+    c_top[...] = wc[:, :, :HALO]
+    c_bottom[...] = wc[:, :, crows - HALO :]
     c_moves = [move(c_top, rc_next, -1, 0), move(c_bottom, rc_prev, 1, 0)]
 
     flane = lax.broadcasted_iota(jnp.int32, (rows, LANES), 1)
     clane = lax.broadcasted_iota(jnp.int32, (crows, LANES), 1)
-
-    def pack(m, carry):
-        fl, fr, cl, cr = carry
+    fl = fr = jnp.zeros((rows, LANES), F32)
+    cl = cr = jnp.zeros((crows, LANES), F32)
+    for m in range(total):
         for level in range(levels):
             at = PASSES * (m * levels + level)
-            fmask = (flane >= at) & (flane < at + PASSES)
-            cmask = (clane >= at) & (clane < at + PASSES)
-            fl = jnp.where(fmask, pltpu.roll(wf[m, level, :, :LANES], at, 1), fl)
-            fr = jnp.where(fmask, pltpu.roll(wf[m, level, :, cols - LANES :], at + PASSES, 1), fr)
+            if m < half:
+                first = p_ref[m, level, :, :LANES] * d_ref[level, :, :LANES]
+                last = p_ref[m, level, :, cols - LANES :] * d_ref[level, :, cols - LANES :]
+            else:
+                first = coef_ref[level, :, :LANES]
+                last = coef_ref[level, :, cols - LANES :]
+            fl = jnp.where(flane >= at, pltpu.roll(first, at, 1) if at else first, fl)
+            fr = jnp.where(flane >= at, pltpu.roll(last, at + PASSES, 1), fr)
             field = wc[m, level]
-            cl = jnp.where(cmask, pltpu.roll(field[:, :LANES], at, 1), cl)
-            cr = jnp.where(cmask, pltpu.roll(field[:, ccols - LANES :], at + PASSES, 1), cr)
-        return fl, fr, cl, cr
-
-    fzero = jnp.zeros((rows, LANES), F32)
-    czero = jnp.zeros((crows, LANES), F32)
-    fl, fr, cl, cr = lax.fori_loop(0, total, pack, (fzero, fzero, czero, czero))
+            cl = jnp.where(
+                clane >= at, pltpu.roll(field[:, :LANES], at, 1) if at else field[:, :LANES], cl
+            )
+            cr = jnp.where(clane >= at, pltpu.roll(field[:, ccols - LANES :], at + PASSES, 1), cr)
     for side, (fine, small) in enumerate(((fl, cl), (fr, cr))):
         strips[side, 0:crows] = small
         strips[side, crows : crows + rows] = fine
@@ -220,8 +235,17 @@
         dy = 2 * side - 1
         other = 1 - side
         y_moves.append(move(strips.at[side, pl.ds(0, crows + rows)], ry.at[other], 0, dy))
-        y_moves.append(move(strips.at[side, pl.ds(0, 16)], rd.at[other, 1], -1, dy))
-        y_moves.append(move(strips.at[side, pl.ds(crows + rows - 8, 16)], rd.at[other, 0], 1, dy))
+        y_moves.append(move(strips.at[side, pl.ds(0, crows + 8)], rd.at[other, 1], -1, dy))
+        y_moves.append(
+            move(strips.at[side, pl.ds(crows + rows - 8, crows + 8)], rd.at[other, 0], 1, dy)
+        )
+
+    spread = jnp.where(
+        lax.broadcasted_iota(jnp.int32, (ccols, cols), 1) // RATIO
+        == lax.broadcasted_iota(jnp.int32, (ccols, cols), 0),
+        1.0, 0.0,
+    ).astype(BF16)
+    acc[...] = jnp.zeros_like(acc)
 
     for slot in y_moves:
         arrive(slot)
@@ -231,9 +255,13 @@
     near = lax.broadcasted_iota(jnp.int32, (8, LANES), 0) < HALO
     for side in (0, 1):
         hyc[side, 0:crows] = ry[side, 0:crows]
-        hyc[side, crows : crows + 8] = jnp.where(near, rd[side, 1, 0:8], rd[side, 0, 8:16])
+        hyc[side, crows : crows + 8] = jnp.where(
+            near, rd[side, 1, 0:8], rd[side, 0, crows : crows + 8]
+        )
         hy[side, 0:rows] = ry[side, crows : crows + rows]
-        hy[side, rows : rows + 8] = jnp.where(near, rd[side, 1, 8:16], rd[side, 0, 0:8])
+        hy[side, rows : rows + 8] = jnp.where(
+            near, rd[side, 1, crows : crows + 8], rd[side, 0, 0:8]
+        )
 
     def columns(ref, index, height):
         lane = lax.broadcasted_iota(jnp.int32, (height, LANES), 1)
@@ -254,10 +282,8 @@
             wc[m, level], rc_next[m, level], rc_prev[m, level], hyc, m * levels + level
         )
 
-    def fine_field(m, level):
-        return extended(
-            wf[m, level], rx_next[m, level], rx_prev[m, level], hy, m * levels + level
-        )
+    def fine_field(m, level, main):
+        return extended(main, rx_next[m, level], rx_prev[m, level], hy, m * levels + level)
 
     ends = [
         value.astype(jnp.int32)
@@ -268,30 +294,27 @@
     ):
         coarse_weights[k] = value
 
-    spread = jnp.where(
-        lax.broadcasted_iota(jnp.int32, (ccols, cols), 1) // RATIO
-        == lax.broadcasted_iota(jnp.int32, (ccols, cols), 0),
-        1.0, 0.0,
-    ).astype(BF16)
-
-    def coarse_member(m, carry):
-        for level in range(levels):
-            u = apply_passes(coarse_field(m, level), [coarse_weights.at[k] for k in range(5)])
-            start = pl.multiple_of((m * levels + level) * crows, 8)
-            wc[m, level] = u[:crows, :ccols]
+    def coarse_members(j, carry):
+        for i in range(batch):
+            m = j * batch + i
+            for level in range(levels):
+                u = apply_passes(coarse_field(m, level), [coarse_weights.at[k] for k in range(5)])
+                line[pl.ds(pl.multiple_of((m * levels + level) * crows, 8), crows)] = u[
+                    :crows, :ccols
+                ]
         return carry
 
-    lax.fori_loop(0, half, coarse_member, 0)
-    lanes_out[...] = split_dot(
-        wc[pl.ds(0, half)].reshape(half * levels * crows, ccols), spread
-    )
-
-    acc[...] = jnp.zeros_like(acc)
+    lax.fori_loop(0, half // batch, coarse_members, 0)
+    lanes_out[...] = split_dot(line[pl.ds(0, count)], spread)
+
     upper = lax.broadcasted_iota(jnp.int32, (2 * RATIO, cols), 0) < RATIO
 
     def fine_member(m, carry):
         for level in range(levels):
-            u = apply_passes(fine_field(m, level), [fine_weights.at[k] for k in range(5)])
+            u = apply_passes(
+                fine_field(m, level, p_ref[m, level] * d_ref[level]),
+                [fine_weights.at[k] for k in range(5)],
+            )
             u = u[:rows, :cols]
             base = (m * levels + level) * crows
             for t in range(rows // (2 * RATIO)):
@@ -306,7 +329,10 @@
         arrive(second)
         if k == 0:
             for j, value in enumerate(
-                stencil_weights(fine_field(half, 0), fine_field(half, 1), rows, cols, *ends)
+                stencil_weights(
+                    fine_field(half, 0, coef_ref[0]), fine_field(half, 1, coef_ref[1]),
+                    rows, cols, *ends
+                )
             ):
                 fine_weights[j] = value
         lax.fori_loop(low, min(high, half), fine_member, 0)
@@ -316,6 +342,7 @@
         recv_sem=recv_sem.at[len(moves)], device_id={"ma": 1 - ma}, device_id_type=MESH,
     )
     swap.start()
+    loads[3].wait()
     swap.wait_recv()
     d, r = d_ref[...], r_ref[...]
     q = d + (acc[...] + acc_other[...]) / (MEMBERS - 1)
@@ -350,26 +377,20 @@
             device_id={"gx": k // n_y, "gy": k % n_y}, device_id_type=MESH,
         )
 
-    def each_peer(action):
-        def body(k, carry):
-            @pl.when(k != me)
-            def _():
-                action(k)
-            return carry
-
-        lax.fori_loop(0, group, body, 0)
-
     each_peer(lambda k: to_peer(k).start())
-    each_peer(lambda k: from_peer(k).wait_recv())
-    summed = jnp.sum(slots[...], axis=0)
-    sums_ref[...] = jnp.broadcast_to(jnp.sum(summed, axis=1, keepdims=True), (8, LANES))
-
-    each_peer(lambda k: to_peer(k).wait_send())
     swap.wait_send()
     for copy, sends, _ in moves:
         @pl.when(sends)
         def _():
             copy.wait_send()
+    each_peer(lambda k: from_peer(k).wait_recv())
+    sums = jnp.sum(jnp.sum(slots[...], axis=0), axis=1, keepdims=True)
+    norm_old, curvature, cross, image = (sums[k : k + 1] for k in range(4))
+    step_length = norm_old / curvature
+    norm_new = norm_old + step_length * (step_length * image - 2.0 * cross)
+    step_ref[...] = jnp.broadcast_to(step_length, (1, cols))
+    growth_ref[...] = jnp.broadcast_to(norm_new / norm_old, (1, cols))
+    each_peer(lambda k: to_peer(k).wait_send())
 
 
 def local(n_x, n_y, perturbations, coefficients, coarse_coefficients, iterate, residual, direction):
@@ -379,16 +400,21 @@
     group = n_x * n_y
     n_moves = 2 * CHUNKS + 2 + 6 + 1
     vmem = pl.BlockSpec(memory_space=pltpu.VMEM)
-    q, sums = pl.pallas_call(
+    q, step_length, growth = pl.pallas_call(
         functools.partial(kernel, (n_x, n_y)),
         out_shape=(
             jax.ShapeDtypeStruct((levels, rows, cols), F32),
-            jax.ShapeDtypeStruct((8, LANES), F32),
+            jax.ShapeDtypeStruct((1, cols), F32),
+            jax.ShapeDtypeStruct((1, cols), F32),
         ),
-        in_specs=[vmem] * 5,
-        out_specs=(vmem, vmem),
+        in_specs=[pl.BlockSpec(memory_space=pltpu.HBM)] * 5,
+        out_specs=(vmem, vmem, vmem),
         scratch_shapes=[
-            pltpu.VMEM((total, levels, rows, cols), F32),
+            pltpu.VMEM((half, levels, rows, cols), F32),
+            pltpu.VMEM((2, rows, cols), F32),
+            pltpu.VMEM((2, crows, ccols), F32),
+            pltpu.VMEM((levels, rows, cols), F32),
+            pltpu.VMEM((levels, rows, cols), F32),
             pltpu.VMEM((total, levels, crows, ccols), F32),
             pltpu.VMEM((half * levels * rows, ccols), F32),
             pltpu.VMEM((half * levels * crows, cols), F32),
@@ -402,7 +428,7 @@
             pltpu.VMEM((total, levels, HALO, ccols), F32),
             pltpu.VMEM((total, levels, HALO, ccols), F32),
             pltpu.VMEM((2, rows + crows, LANES), F32),
-            pltpu.VMEM((2, 2, 16, LANES), F32),
+            pltpu.VMEM((2, 2, crows + 8, LANES), F32),
             pltpu.VMEM((2, rows + 2 * HALO, LANES), F32),
             pltpu.VMEM((2, crows + 2 * HALO, LANES), F32),
             pltpu.VMEM((5, rows + 2 * HALO, cols + LANES), F32),
@@ -411,21 +437,19 @@
             pltpu.VMEM((levels, rows, cols), F32),
             pltpu.VMEM((8, LANES), F32),
             pltpu.VMEM((group, 8, LANES), F32),
+            pltpu.SemaphoreType.DMA((4 + CHUNKS,)),
             pltpu.SemaphoreType.DMA((n_moves,)),
             pltpu.SemaphoreType.DMA((n_moves,)),
             pltpu.SemaphoreType.DMA((group,)),
             pltpu.SemaphoreType.DMA((group,)),
         ],
         compiler_params=pltpu.CompilerParams(
-            collective_id=0, has_side_effects=True, vmem_limit_bytes=48 << 20
+            collective_id=0, has_side_effects=True, vmem_limit_bytes=62 << 20
         ),
     )(perturbations, coefficients, coarse_coefficients, residual, direction)
-    norm_old, curvature, cross, image = (sums[k, 0] for k in range(4))
-    step_length = norm_old / curvature
-    norm_new = norm_old + step_length * (step_length * image - 2.0 * cross)
     new_iterate = iterate + step_length * direction
     new_residual = residual - step_length * q
-    new_direction = new_residual + norm_new / norm_old * direction
+    new_direction = new_residual + growth * direction
     return (new_iterate, new_residual, new_direction)
 
 

time: 45.7 us -> 34.9 us (0.76)
  local copies, waits for them, and re-layouts: 5.51 us -> 0.01 us
  between operations: 4.61 us -> 0.69 us
  Pallas kernels: 34.5 us -> 32.2 us
  other arithmetic: 0.78 us -> 1.69 us
    unnamed x16 -> x6, local copies, waits for them, and re-layouts: 4.96 us -> 0.01 us
    pallas_call x1, Pallas kernels: 34.5 us -> 32.2 us  [local(): pl.pallas_call(functools.partial(kernel, (n_x, n_y)), out_shape=(jax.Shap...]
    add x1, other arithmetic: 0.78 us -> 1.69 us  [local(): new_direction = new_residual + growth * direction]
    slice x1 -> x0, local copies, waits for them, and re-layouts: 0.55 us -> none  [local(): norm_old, curvature, cross, image = (sums[k, 0] for k in range(4))]
where the time goes in v2:
time: 34.9 us; the launch traced here: 34.6 us
  Pallas kernels  32.2 us (92%)
  other arithmetic  1.69 us (5%)
  between operations  0.69 us (2%)
    pallas_call x1, Pallas kernels, local(): pl.pallas_call(functools.partial(kernel, (n_x, n_y)), out_shape=(jax.Shap...  32.2 us
    add x1, other arithmetic, local(): new_direction = new_residual + growth * direction  1.69 us

profile of v2, /device:TPU:0, one launch (start us, length us, event | category | flops | bytes accessed | tf_op | source)
XLA Modules:
  0.0 34.6 jit_solution(10634133615417987257)
XLA Ops:
  0.6 0.0 copy-start
  0.6 0.0 copy-start.1
  0.7 0.0 copy-start.2
  0.7 32.2 %shard_map.85 = (f32[2,32,512]{2,1,0:T(8,128)}, f32[1,512]{1,0:T(1,128)}, f32[1,512]{1,0:T(1,128)}) custom-call(f32[15,2,32,512]{3,2,1,0:T(8,128)} %p_hbm.1, f32[2,32,512]{2,1,0:T(8,128)} %coef_hbm.1, f32[2,8,128]{2,1,0:T(8,128)} %ccoef_hbm.1, f32[2,32,512]{2,1,0:T(8,128)} %r_hbm.1, f32[2,32,512]{2,1,0:T(8,128)} %d_hbm.1), custom_call_target="tpu_custom_call" | custom-call | tf_op jit(solution)/shard_map/pallas_call | solution.py:403
  32.9 0.0 copy-done
  32.9 0.0 copy-done.1
  32.9 0.0 copy-done.2
  32.9 1.7 %multiply_add_fusion = (f32[2,32,512]{2,1,0:T(8,128)}, f32[2,32,512]{2,1,0:T(8,128)}, f32[2,32,512]{2,1,0:T(8,128)}) fusion(f32[2,32,512]{2,1,0:T(8,128)S(1)} %copy-done, f32[512]{0:T(512)} %bitcast.3, f32[2,32,512]{2,1,0:T(8,128)S(1)} %copy-done.1, f32[2,32,512]{2,1,0:T(8,128)} %get-tuple-element.7, f32[512]{0:T(512)} %bitcast.2, f32[2,32,512]{2,1,0:T(8,128)S(1)} %copy-done.2), kind=kLoop, calls=%fused_computation | loop fusion | flops 196608 | bytes 921600 | tf_op jit(solution)/shard_map/add | solution.py:452
Async XLA Ops:
  0.6 32.3 %copy-start = (f32[2,32,512]{2,1,0:T(8,128)S(1)}, f32[2,32,512]{2,1,0:T(8,128)}, u32[]{:S(2)}) copy-start(f32[2,32,512]{2,1,0:T(8,128)} %d_hbm.1) | copy-start | bytes 393220
  0.6 32.3 %copy-start.1 = (f32[2,32,512]{2,1,0:T(8,128)S(1)}, f32[2,32,512]{2,1,0:T(8,128)}, u32[]{:S(2)}) copy-start(f32[2,32,512]{2,1,0:T(8,128)} %r_hbm.1) | copy-start | bytes 393220
  0.7 32.3 %copy-start.2 = (f32[2,32,512]{2,1,0:T(8,128)S(1)}, f32[2,32,512]{2,1,0:T(8,128)}, u32[]{:S(2)}) copy-start(f32[2,32,512]{2,1,0:T(8,128)} %param.9) | copy-start | bytes 393220

commit v3 on v2

--- a/solution.py
+++ b/solution.py
@@ -96,14 +96,6 @@
 
         lax.fori_loop(1, group, body, 0, unroll=group <= 16)
 
-    barrier = pltpu.get_barrier_semaphore()
-    pl.semaphore_signal(barrier, inc=1, device_id={"ma": 1 - ma}, device_id_type=MESH)
-    each_peer(
-        lambda k: pl.semaphore_signal(
-            barrier, inc=1, device_id={"gx": k // n_y, "gy": k % n_y}, device_id_type=MESH
-        )
-    )
-
     total = half + 1
     bounds = [total - (total * k) // CHUNKS for k in range(CHUNKS + 1)]
     loads = [
@@ -119,6 +111,14 @@
         )
     for k in (0, 1, 4, 5, 6, 7, 2, 3):
         loads[k].start()
+
+    barrier = pltpu.get_barrier_semaphore()
+    pl.semaphore_signal(barrier, inc=1, device_id={"ma": 1 - ma}, device_id_type=MESH)
+    each_peer(
+        lambda k: pl.semaphore_signal(
+            barrier, inc=1, device_id={"gx": k // n_y, "gy": k % n_y}, device_id_type=MESH
+        )
+    )
 
     def zero_if(absent, ref):
         @pl.when(absent)
@@ -164,23 +164,12 @@
     loads[1].wait()
     x_top[half] = coef_ref[:, :HALO]
     x_bottom[half] = coef_ref[:, rows - HALO :]
-    x_moves = []
     for k in range(CHUNKS):
         low, high = bounds[k + 1], bounds[k]
         loads[4 + k].wait()
         for m in range(low, min(high, half)):
             x_top[m] = p_ref[m, :, :HALO] * d_ref[:, :HALO]
             x_bottom[m] = p_ref[m, :, rows - HALO :] * d_ref[:, rows - HALO :]
-        if k == 0:
-            pl.semaphore_wait(barrier, group)
-        span = pl.ds(low, high - low)
-        x_moves.append(
-            (
-                move(x_top.at[span], rx_next.at[span], -1, 0),
-                move(x_bottom.at[span], rx_prev.at[span], 1, 0),
-                low, high,
-            )
-        )
 
     pick = lax.broadcasted_iota(jnp.int32, (cols, ccols), 0) // RATIO
     gather = jnp.where(
@@ -204,7 +193,6 @@
     wc[half] = ccoef_ref[...]
     c_top[...] = wc[:, :, :HALO]
     c_bottom[...] = wc[:, :, crows - HALO :]
-    c_moves = [move(c_top, rc_next, -1, 0), move(c_bottom, rc_prev, 1, 0)]
 
     flane = lax.broadcasted_iota(jnp.int32, (rows, LANES), 1)
     clane = lax.broadcasted_iota(jnp.int32, (crows, LANES), 1)
@@ -230,6 +218,7 @@
         strips[side, 0:crows] = small
         strips[side, crows : crows + rows] = fine
         strips[side, crows + rows :] = small
+    pl.semaphore_wait(barrier, group)
     y_moves = []
     for side in (0, 1):
         dy = 2 * side - 1
@@ -238,6 +227,19 @@
         y_moves.append(move(strips.at[side, pl.ds(0, crows + 8)], rd.at[other, 1], -1, dy))
         y_moves.append(
             move(strips.at[side, pl.ds(crows + rows - 8, crows + 8)], rd.at[other, 0], 1, dy)
+        )
+
+    c_moves = [move(c_top, rc_next, -1, 0), move(c_bottom, rc_prev, 1, 0)]
+    x_moves = []
+    for k in range(CHUNKS):
+        low, high = bounds[k + 1], bounds[k]
+        span = pl.ds(low, high - low)
+        x_moves.append(
+            (
+                move(x_top.at[span], rx_next.at[span], -1, 0),
+                move(x_bottom.at[span], rx_prev.at[span], 1, 0),
+                low, high,
+            )
         )
 
     spread = jnp.where(

time: 34.9 us -> 30.8 us (0.88)
  Pallas kernels: 32.2 us -> 28.2 us
    pallas_call x1, Pallas kernels: 32.2 us -> 28.2 us  [local(): pl.pallas_call(functools.partial(kernel, (n_x, n_y)), out_shape=(jax.Shap...]
where the time goes in v3:
time: 30.8 us; the launch traced here: 30.6 us
  Pallas kernels  28.2 us (92%)
  other arithmetic  1.69 us (5%)
  between operations  0.69 us (2%)
    pallas_call x1, Pallas kernels, local(): pl.pallas_call(functools.partial(kernel, (n_x, n_y)), out_shape=(jax.Shap...  28.2 us
    add x1, other arithmetic, local(): new_direction = new_residual + growth * direction  1.69 us

profile of v3, /device:TPU:0, one launch (start us, length us, event | category | flops | bytes accessed | tf_op | source)
XLA Modules:
  0.0 30.6 jit_solution(1246604565596641138)
XLA Ops:
  0.6 0.0 copy-start
  0.6 0.0 copy-start.1
  0.7 0.0 copy-start.2
  0.7 28.2 %shard_map.85 = (f32[2,32,512]{2,1,0:T(8,128)}, f32[1,512]{1,0:T(1,128)}, f32[1,512]{1,0:T(1,128)}) custom-call(f32[15,2,32,512]{3,2,1,0:T(8,128)} %p_hbm.1, f32[2,32,512]{2,1,0:T(8,128)} %coef_hbm.1, f32[2,8,128]{2,1,0:T(8,128)} %ccoef_hbm.1, f32[2,32,512]{2,1,0:T(8,128)} %r_hbm.1, f32[2,32,512]{2,1,0:T(8,128)} %d_hbm.1), custom_call_target="tpu_custom_call" | custom-call | tf_op jit(solution)/shard_map/pallas_call | solution.py:405
  28.9 0.0 copy-done
  28.9 0.0 copy-done.1
  28.9 0.0 copy-done.2
  28.9 1.7 %multiply_add_fusion = (f32[2,32,512]{2,1,0:T(8,128)}, f32[2,32,512]{2,1,0:T(8,128)}, f32[2,32,512]{2,1,0:T(8,128)}) fusion(f32[2,32,512]{2,1,0:T(8,128)S(1)} %copy-done, f32[512]{0:T(512)} %bitcast.3, f32[2,32,512]{2,1,0:T(8,128)S(1)} %copy-done.1, f32[2,32,512]{2,1,0:T(8,128)} %get-tuple-element.7, f32[512]{0:T(512)} %bitcast.2, f32[2,32,512]{2,1,0:T(8,128)S(1)} %copy-done.2), kind=kLoop, calls=%fused_computation | loop fusion | flops 196608 | bytes 921600 | tf_op jit(solution)/shard_map/add | solution.py:454
Async XLA Ops:
  0.6 28.3 %copy-start = (f32[2,32,512]{2,1,0:T(8,128)S(1)}, f32[2,32,512]{2,1,0:T(8,128)}, u32[]{:S(2)}) copy-start(f32[2,32,512]{2,1,0:T(8,128)} %d_hbm.1) | copy-start | bytes 393220
  0.6 28.3 %copy-start.1 = (f32[2,32,512]{2,1,0:T(8,128)S(1)}, f32[2,32,512]{2,1,0:T(8,128)}, u32[]{:S(2)}) copy-start(f32[2,32,512]{2,1,0:T(8,128)} %r_hbm.1) | copy-start | bytes 393220
  0.7 28.3 %copy-start.2 = (f32[2,32,512]{2,1,0:T(8,128)S(1)}, f32[2,32,512]{2,1,0:T(8,128)}, u32[]{:S(2)}) copy-start(f32[2,32,512]{2,1,0:T(8,128)} %param.9) | copy-start | bytes 393220

commit v4 on v3

--- a/solution.py
+++ b/solution.py
@@ -312,12 +312,19 @@
     upper = lax.broadcasted_iota(jnp.int32, (2 * RATIO, cols), 0) < RATIO
 
     def fine_member(m, carry):
+        fields = jnp.stack(
+            [fine_field(m, level, p_ref[m, level] * d_ref[level]) for level in range(levels)]
+        )
+        for _ in range(PASSES):
+            fields = (
+                fine_weights[0][None] * fields
+                + fine_weights[1][None] * shift_up(fields, 1)
+                + fine_weights[2][None] * shift_down(fields, 1)
+                + fine_weights[3][None] * shift_up(fields, 2)
+                + fine_weights[4][None] * shift_down(fields, 2)
+            )
         for level in range(levels):
-            u = apply_passes(
-                fine_field(m, level, p_ref[m, level] * d_ref[level]),
-                [fine_weights.at[k] for k in range(5)],
-            )
-            u = u[:rows, :cols]
+            u = fields[level, :rows, :cols]
             base = (m * levels + level) * crows
             for t in range(rows // (2 * RATIO)):
                 a = jnp.broadcast_to(lanes_out[pl.ds(base + 2 * t, 1), :], (2 * RATIO, cols))

time: 30.8 us -> 30.3 us (0.984)
  Pallas kernels: 28.2 us -> 27.7 us
    pallas_call x1, Pallas kernels: 28.2 us -> 27.7 us  [local(): pl.pallas_call(functools.partial(kernel, (n_x, n_y)), out_shape=(jax.Shap...]
where the time goes in v4:
time: 30.3 us; the launch traced here: 30.1 us
  Pallas kernels  27.7 us (91%)
  other arithmetic  1.69 us (6%)
  between operations  0.69 us (2%)
    pallas_call x1, Pallas kernels, local(): pl.pallas_call(functools.partial(kernel, (n_x, n_y)), out_shape=(jax.Shap...  27.7 us
    add x1, other arithmetic, local(): new_direction = new_residual + growth * direction  1.69 us

profile of v4, /device:TPU:0, one launch (start us, length us, event | category | flops | bytes accessed | tf_op | source)
XLA Modules:
  0.0 30.1 jit_solution(978315708018713615)
XLA Ops:
  0.6 0.0 copy-start
  0.6 0.0 copy-start.1
  0.7 0.0 copy-start.2
  0.7 27.7 %shard_map.85 = (f32[2,32,512]{2,1,0:T(8,128)}, f32[1,512]{1,0:T(1,128)}, f32[1,512]{1,0:T(1,128)}) custom-call(f32[15,2,32,512]{3,2,1,0:T(8,128)} %p_hbm.1, f32[2,32,512]{2,1,0:T(8,128)} %coef_hbm.1, f32[2,8,128]{2,1,0:T(8,128)} %ccoef_hbm.1, f32[2,32,512]{2,1,0:T(8,128)} %r_hbm.1, f32[2,32,512]{2,1,0:T(8,128)} %d_hbm.1), custom_call_target="tpu_custom_call" | custom-call | tf_op jit(solution)/shard_map/pallas_call | solution.py:412
  28.3 0.0 copy-done
  28.4 0.0 copy-done.1
  28.4 0.0 copy-done.2
  28.4 1.7 %multiply_add_fusion = (f32[2,32,512]{2,1,0:T(8,128)}, f32[2,32,512]{2,1,0:T(8,128)}, f32[2,32,512]{2,1,0:T(8,128)}) fusion(f32[2,32,512]{2,1,0:T(8,128)S(1)} %copy-done, f32[512]{0:T(512)} %bitcast.3, f32[2,32,512]{2,1,0:T(8,128)S(1)} %copy-done.1, f32[2,32,512]{2,1,0:T(8,128)} %get-tuple-element.7, f32[512]{0:T(512)} %bitcast.2, f32[2,32,512]{2,1,0:T(8,128)S(1)} %copy-done.2), kind=kLoop, calls=%fused_computation | loop fusion | flops 196608 | bytes 921600 | tf_op jit(solution)/shard_map/add | solution.py:461
Async XLA Ops:
  0.6 27.7 %copy-start = (f32[2,32,512]{2,1,0:T(8,128)S(1)}, f32[2,32,512]{2,1,0:T(8,128)}, u32[]{:S(2)}) copy-start(f32[2,32,512]{2,1,0:T(8,128)} %d_hbm.1) | copy-start | bytes 393220
  0.6 27.7 %copy-start.1 = (f32[2,32,512]{2,1,0:T(8,128)S(1)}, f32[2,32,512]{2,1,0:T(8,128)}, u32[]{:S(2)}) copy-start(f32[2,32,512]{2,1,0:T(8,128)} %r_hbm.1) | copy-start | bytes 393220
  0.7 27.7 %copy-start.2 = (f32[2,32,512]{2,1,0:T(8,128)S(1)}, f32[2,32,512]{2,1,0:T(8,128)}, u32[]{:S(2)}) copy-start(f32[2,32,512]{2,1,0:T(8,128)} %param.9) | copy-start | bytes 393220
